TPU v7x, 256 devices: a whole 4x4x8 slice. The times are simulated.
256 devices in a mesh: tm: 256 (over z, y, x, core).
Axes of the slice: x: 4, y: 4, z: 8, core: 2. Of those that a mesh axis runs over, the one named last changes fastest.
Arguments:
- queries: bfloat16 [1024, 32, 640], P('tm'), may hold values from -8 to 8
- keys: bfloat16 [1024, 32, 640], P('tm'), may hold values from -8 to 8
- values: bfloat16 [1024, 32, 640], P('tm'), may hold values from -8 to 8
- out_grad: bfloat16 [1024, 32, 640], P('tm'), may hold values from -8 to 8
- clip_lengths: int32 [128], replicated, may hold values from 1 to 24, 1024 in all
Outputs:
- attended: bfloat16 [1024, 32, 640], P('tm')
- grad_queries: bfloat16 [1024, 32, 640], P('tm')
- grad_keys: bfloat16 [1024, 32, 640], P('tm')
- grad_values: bfloat16 [1024, 32, 640], P('tm')
Inputs may be any that keep to these rules, and one draw needn't show every extreme that they name: `clip_lengths`: lengths sum to 1024; the longest clip has exactly 24 frames.
All inputs are finite; a program needn't handle non-finite values.
Results may differ from a plain program's by a relative error of at most 0.0088.
Values may be sent and summed in bfloat16 or wider, within the bound.
No kernel may reach another device: no remote copies, remote signals or barrier semaphores. Data moves between devices by JAX's collectives and lax.ppermute only.
A program may use at most 64 MiB of HBM per device.

v0:
```python
import jax
import jax.numpy as jnp
from jax import lax
from jax.experimental import pallas as pl
from jax.experimental.pallas import tpu as pltpu
from jax.sharding import PartitionSpec as P


HEADS = 10
F = 4
C = 2 * F
REACH = 3
HALO = C
REMOTE = C + 1
SLOTS = C + 2
SIZE = 64
STEP = 256
SPAN = 384
REST = 256
WIDTH = HEADS * SIZE
F32 = jnp.float32
BF16 = jnp.bfloat16
VMEM = pl.BlockSpec(memory_space=pltpu.VMEM)
SMEM = pl.BlockSpec(memory_space=pltpu.SMEM)
HBM = pl.BlockSpec(memory_space=pltpu.HBM)
LIMIT = pltpu.CompilerParams(vmem_limit_bytes=20 << 20)

OWN, PREV, BACK, OPEN, TAKE, META = 0, C, 2 * C, 2 * C + 1, 2 * C + 2, 2 * C + 2 + REACH


def ring(value, steps):
    count = lax.axis_size("tm")
    return lax.ppermute(value, "tm", [(s, (s + steps) % count) for s in range(count)])


def swap(value):
    count = lax.axis_size("tm")
    return lax.ppermute(value, "tm", [(s, s ^ 1) for s in range(count)])


def place():
    device = lax.axis_index("tm")
    return lax.shift_right_logical(device, 1), device & 1


def window(core):
    return pl.ds(pl.multiple_of(core * STEP, 128), SPAN)


def prep_kernel(lengths_ref, keys_ref, values_ref, meta_ref, mine_ref, send_ref, frames, sems):
    copies = [
        pltpu.make_async_copy(ref, frames.at[i], sems.at[i])
        for i, ref in enumerate((keys_ref, values_ref))
    ]
    for copy in copies:
        copy.start()
    chip, core = place()
    first = chip * C
    total = lax.axis_size("tm") * F
    clips = lengths_ref.shape[1]
    rows = lax.broadcasted_iota(jnp.int32, (clips, clips), 0)
    columns = lax.broadcasted_iota(jnp.int32, (clips, clips), 1)
    earlier = jnp.where(rows < columns, 1.0, 0.0).astype(BF16)
    lengths = jnp.broadcast_to(lengths_ref[...].astype(F32), (16, clips)).astype(BF16)
    starts = jnp.dot(lengths, earlier, preferred_element_type=F32)[:1].astype(jnp.int32)

    def owner_of(frame):
        return jnp.max(jnp.where(starts <= frame, starts, 0))

    owners = [owner_of(first + i) for i in range(C)]
    for i in range(C):
        local = owners[i] - first
        meta_ref[OWN + i] = jnp.where(local >= 0, local, REMOTE)
        meta_ref[PREV + i] = jnp.where(local == i, i, i - 1 if i else HALO)
    meta_ref[BACK] = jnp.clip(chip - lax.shift_right_logical(owners[0], 3), 1, REACH)
    opened = owners[C - 1] - first
    meta_ref[OPEN] = opened
    for k in range(1, REACH + 1):
        ahead = first + C * k
        owner = owner_of(ahead) - first
        mine = (owner >= 0) & (owner < C) & (ahead < total)
        meta_ref[TAKE + k - 1] = mine.astype(jnp.int32)
    local = opened - core * F
    holds = (local >= 0) & (local < F)
    frame = jnp.clip(local, 0, F - 1)
    for copy in copies:
        copy.wait()
    for target, columns in ((mine_ref, window(core)), (send_ref, window(1 - core))):
        for i in range(2):
            target[i] = jnp.where(holds, frames[i, frame, :, columns], 0).astype(BF16)
            target[2 + i] = jnp.where(core == 1, frames[i, F - 1, :, columns], 0).astype(BF16)


def pack_kernel(q_ref, keys_ref, values_ref, g_ref, after_ref, mine_ref, send_ref, sems):
    core = place()[1]
    copies = []
    for t, (target, side) in enumerate(((send_ref, 1 - core), (mine_ref, core))):
        for i, ref in enumerate((q_ref, keys_ref, values_ref, g_ref)):
            copies.append(
                pltpu.make_async_copy(
                    ref.at[:, :, window(side)], target.at[pl.ds(i * F, F)], sems.at[4 * t + i]
                )
            )
    for copy in copies:
        copy.start()
    for copy in copies:
        copy.wait()


def gather_slots(meta_ref, mine_ref, theirs_ref, received, q, keys, values, g):
    core = place()[1]
    for source, base in ((mine_ref, core * F), (theirs_ref, (1 - core) * F)):
        for i, target in enumerate((q, keys, values, g)):
            for j in range(F):
                target[base + j] = source[i * F + j]
    keys[HALO] = received[0][2]
    values[HALO] = received[0][3]
    back = meta_ref[BACK]
    for k in range(1, REACH + 1):

        @pl.when(back == k)
        def _():
            keys[REMOTE] = received[k - 1][0]
            values[REMOTE] = received[k - 1][1]


def spread(block):
    lane = lax.broadcasted_iota(jnp.int32, block.shape, 1)
    parts = [
        jnp.where((lane >= start) & (lane < start + SIZE), block, jnp.zeros_like(block))
        for start in range(0, block.shape[1], SIZE)
    ]
    return jnp.concatenate(parts, axis=0)


def fold(product):
    heads = product.shape[1] // SIZE
    tokens = product.shape[0] // heads
    lane = lax.broadcasted_iota(jnp.int32, (tokens, product.shape[1]), 1)
    result = product[:tokens]
    for h in range(1, heads):
        result = jnp.where(lane < h * SIZE, result, product[h * tokens : (h + 1) * tokens])
    return result


def contract(a, b, da, db):
    return lax.dot_general(a, b, (((da,), (db,)), ((), ())), preferred_element_type=F32)


def soft(keys, values, q, g):
    scale = SIZE ** (-0.5)
    scores = contract(keys, q, 1, 1) * scale
    grad_prob = contract(values, g, 1, 1)
    expos = jnp.exp(scores - jnp.max(scores, axis=0, keepdims=True))
    prob = expos / jnp.sum(expos, axis=0, keepdims=True)
    inner = jnp.sum(prob * grad_prob, axis=0, keepdims=True)
    grad_score = prob * (grad_prob - inner) * scale
    return prob.astype(BF16), grad_score.astype(BF16)


GROUPS = tuple(
    slice(start, min(start + 4 * SIZE, SPAN)) for start in range(0, SPAN, 4 * SIZE)
)


def pair(slots, own, prev, columns):
    return jnp.concatenate([slots[own, :, columns], slots[prev, :, columns]], axis=0)


def near_kernel(meta_ref, mine_ref, theirs_ref, r1, r2, r3, sums_ref, edge_ref, q, keys, values, g):
    gather_slots(meta_ref, mine_ref, theirs_ref, (r1, r2, r3), q, keys, values, g)
    tokens = q.shape[1]
    for columns in GROUPS:
        span = columns.stop - columns.start
        key_total = jnp.zeros((tokens, span), F32)
        value_total = jnp.zeros((tokens, span), F32)
        for i in range(C):
            own, prev = meta_ref[OWN + i], meta_ref[PREV + i]
            heads_q, heads_g = spread(q[i, :, columns]), spread(g[i, :, columns])
            prob, grad_score = soft(
                pair(keys, own, prev, columns), pair(values, own, prev, columns), heads_q, heads_g
            )
            rows = 2 * tokens if i == 0 else tokens
            grad_value = contract(prob[:rows], heads_g, 1, 0)
            grad_key = contract(grad_score[:rows], heads_q, 1, 0)
            remote = own == REMOTE
            key_total += jnp.where(remote, grad_key[:tokens], 0.0)
            value_total += jnp.where(remote, grad_value[:tokens], 0.0)
            if i == 0:
                halo = prev == HALO
                edge_ref[2, :, columns] = jnp.where(halo, grad_key[tokens:], 0.0).astype(BF16)
                edge_ref[3, :, columns] = jnp.where(halo, grad_value[tokens:], 0.0).astype(BF16)
        for target in (sums_ref, edge_ref):
            target[0, :, columns] = key_total.astype(BF16)
            target[1, :, columns] = value_total.astype(BF16)


def full_kernel(meta_ref, mine_ref, theirs_ref, r1, r2, r3, after_ref, keep_ref, send_ref, touch_ref, *scratch):
    q, keys, values, g, key_sum, value_sum, out = scratch
    gather_slots(meta_ref, mine_ref, theirs_ref, (r1, r2, r3), q, keys, values, g)
    key_sum[...] = jnp.zeros_like(key_sum)
    value_sum[...] = jnp.zeros_like(value_sum)
    tokens = q.shape[1]
    for i in range(C):
        own, prev = meta_ref[OWN + i], meta_ref[PREV + i]
        for columns in GROUPS:
            heads_q, heads_g = spread(q[i, :, columns]), spread(g[i, :, columns])
            key = pair(keys, own, prev, columns)
            value = pair(values, own, prev, columns)
            prob, grad_score = soft(key, value, heads_q, heads_g)
            out[i, :, columns] = fold(contract(prob, value, 0, 0)).astype(BF16)
            out[C + i, :, columns] = fold(contract(grad_score, key, 0, 0)).astype(BF16)
            grad_value = contract(prob, heads_g, 1, 0)
            grad_key = contract(grad_score, heads_q, 1, 0)
            key_sum[own, :, columns] += grad_key[:tokens]
            value_sum[own, :, columns] += grad_value[:tokens]
            key_sum[prev, :, columns] += grad_key[tokens:]
            value_sum[prev, :, columns] += grad_value[tokens:]
    for i in range(C):
        out[2 * C + i] = key_sum[i].astype(BF16)
        out[3 * C + i] = value_sum[i].astype(BF16)
    opened = jnp.maximum(meta_ref[OPEN], 0)
    touch_ref[0] = key_sum[opened]
    touch_ref[1] = value_sum[opened]
    touch_ref[2] = key_sum[C - 1]
    touch_ref[3] = value_sum[C - 1]
    core = place()[1]
    lacking = pl.ds(pl.multiple_of(core * 128, 128), REST)
    for a in range(4):
        for j in range(F):
            keep_ref[a * F + j] = out[a * C + core * F + j]
            send_ref[a * F + j] = out[a * C + (1 - core) * F + j, :, lacking]


def join(core, target, kept, got):
    @pl.when(core == 0)
    def _():
        target[:, :SPAN] = kept
        target[:, SPAN:] = got

    @pl.when(core == 1)
    def _():
        target[:, :STEP] = got
        target[:, STEP:] = kept


def early_kernel(keep_ref, got_ref, attended_ref, grad_q_ref):
    core = place()[1]
    for a, target in enumerate((attended_ref, grad_q_ref)):
        for j in range(F):
            join(core, target.at[j], keep_ref[a * F + j], got_ref[a * F + j])


def touch_kernel(meta_ref, touch_ref, r1, r2, r3, kept_ref, send_ref):
    core = place()[1]
    lacking = pl.ds(pl.multiple_of(core * 128, 128), REST)
    same = meta_ref[OPEN] == C - 1
    for a in range(2):
        edge = r1[2 + a].astype(F32)
        total = touch_ref[a] + jnp.where(same, edge, 0.0)
        for k, r in enumerate((r1, r2, r3)):
            total += jnp.where(meta_ref[TAKE + k] > 0, r[a].astype(F32), 0.0)
        kept_ref[a] = total.astype(BF16)
        kept_ref[2 + a] = (touch_ref[2 + a] + edge).astype(BF16)
    for a in range(4):
        send_ref[a] = kept_ref[a, :, lacking]


def final_kernel(meta_ref, keep_ref, got_ref, touched_ref, touched_got_ref, grad_keys_ref, grad_values_ref):
    core = place()[1]
    local = meta_ref[OPEN] - core * F
    for a, target in enumerate((grad_keys_ref, grad_values_ref)):
        for j in range(F):
            join(core, target.at[j], keep_ref[(2 + a) * F + j], got_ref[(2 + a) * F + j])

        @pl.when(core == 1)
        def _():
            join(core, target.at[F - 1], touched_ref[2 + a], touched_got_ref[2 + a])

        @pl.when((local >= 0) & (local < F))
        def _():
            join(core, target.at[local], touched_ref[a], touched_got_ref[a])


def call(kernel, operands, outs, in_specs, out_specs, scratch=(), flops=0, size=0):
    return pl.pallas_call(
        kernel,
        out_shape=outs,
        in_specs=in_specs,
        out_specs=out_specs,
        scratch_shapes=list(scratch),
        compiler_params=LIMIT,
        cost_estimate=pl.CostEstimate(flops=flops, bytes_accessed=size, transcendentals=0),
    )(*operands)


def step(queries, keys, values, out_grad, clip_lengths):
    tokens = queries.shape[1]
    queries, keys, values, out_grad = (
        pltpu.with_memory_space_constraint(a, pltpu.HBM) for a in (queries, keys, values, out_grad)
    )

    def shape(count, columns, dtype=BF16):
        return jax.ShapeDtypeStruct((count, tokens, columns), dtype)

    def room(count, dtype=BF16):
        return pltpu.VMEM((count, tokens, SPAN), dtype)

    meta, own_edge, send_edge = call(
        prep_kernel,
        (clip_lengths.reshape(1, -1), keys, values),
        (jax.ShapeDtypeStruct((META,), jnp.int32), shape(4, SPAN), shape(4, SPAN)),
        [VMEM, HBM, HBM],
        (SMEM, VMEM, VMEM),
        [pltpu.VMEM((2, F, tokens, WIDTH), BF16), pltpu.SemaphoreType.DMA((2,))],
        size=1 << 20,
    )
    got_edge = swap(send_edge)
    edge = own_edge + got_edge
    opened = own_edge[:2] + got_edge[:2]
    far = ring(opened, 6), ring(opened, 4)
    received = (ring(edge, 2), far[1], far[0])
    mine, send = call(
        pack_kernel,
        (queries, keys, values, out_grad, edge),
        (shape(4 * F, SPAN), shape(4 * F, SPAN)),
        [HBM] * 4 + [VMEM],
        (VMEM, VMEM),
        [pltpu.SemaphoreType.DMA((8,))],
        size=2 << 20,
    )
    theirs = swap(send)
    slots = [room(C), room(SLOTS), room(SLOTS), room(C)]
    operands = (meta, mine, theirs, *received)
    flops = 24 * C * tokens * tokens * SPAN
    sums, edge_sums = call(
        near_kernel,
        operands,
        (shape(2, SPAN), shape(4, SPAN)),
        [SMEM] + [VMEM] * 5,
        (VMEM, VMEM),
        slots,
        flops,
        2 << 20,
    )
    far = ring(sums, -6), ring(sums, -4)
    returned = (ring(edge_sums, -2), far[1], far[0])
    keep, send_out, touch = call(
        full_kernel,
        (*operands, sums),
        (shape(4 * F, SPAN), shape(4 * F, REST), shape(4, SPAN, F32)),
        [SMEM] + [VMEM] * 6,
        (VMEM,) * 3,
        slots + [room(SLOTS, F32), room(SLOTS, F32), room(4 * C)],
        4 * flops,
        4 << 20,
    )
    got_out = swap(send_out)
    attended, grad_queries = call(
        early_kernel, (keep, got_out), (shape(F, WIDTH),) * 2, [VMEM] * 2, (VMEM,) * 2, size=1 << 20
    )
    touched, send_touched = call(
        touch_kernel,
        (meta, touch, *returned),
        (shape(4, SPAN), shape(4, REST)),
        [SMEM] + [VMEM] * 4,
        (VMEM,) * 2,
        size=1 << 20,
    )
    grad_keys, grad_values = call(
        final_kernel,
        (meta, keep, got_out, touched, swap(send_touched)),
        (shape(F, WIDTH),) * 2,
        [SMEM] + [VMEM] * 4,
        (VMEM,) * 2,
        size=1 << 20,
    )
    return attended, grad_queries, grad_keys, grad_values


def solution(mesh):
    sharded = P("tm", None, None)
    return jax.shard_map(
        step,
        mesh=mesh,
        in_specs=(sharded,) * 4 + (P(),),
        out_specs=(sharded,) * 4,
        check_vma=False,
    )
```

profile of v0, /device:TPU:1, one launch (start us, length us, event | category | flops | bytes accessed | tf_op | source)
XLA Modules:
  0.0 44.3 jit_solution(2106328023728489355)
XLA Ops:
  0.6 0.0 copy-start
  0.6 0.6 %copy-done = s32[128]{0:T(128)S(1)} copy-done((s32[128]{0:T(128)S(1)}, s32[128]{0:T(128)}, u32[]{:S(2)}) %copy-start) | copy-done | bytes 536
  1.3 1.6 %shard_map.84 = (s32[21]{0:T(128)S(1)}, bf16[4,32,384]{2,1,0:T(8,128)(2,1)S(1)}, bf16[4,32,384]{2,1,0:T(8,128)(2,1)S(1)}) custom-call(s32[1,128]{1,0:T(1,128)S(1)} %bitcast.1, bf16[4,32,640]{2,1,0:T(8,128)(2,1)} %keys_ref.3, bf16[4,32,640]{2,1,0:T(8,128)(2,1)} %values_ref.3), custom_call_target="tpu_custom_call" | custom-call | bytes 1048576 | tf_op jit(solution)/shard_map/pallas_call | solution.py:286
  2.9 3.3 %collective-permute-start = (bf16[4,32,384]{2,1,0:T(8,128)(2,1)S(1)}, bf16[4,32,384]{2,1,0:T(8,128)(2,1)S(1)}, u32[]{:S(2)}, u32[]{:S(2)}) collective-permute-start(bf16[4,32,384]{2,1,0:T(8,128)(2,1)S(1)} %get-tuple-element.22), channel_id=1, source_target_pairs={{0,1},{1,0},{2,3},{3,2},{4,5},{5,4},{6,7},{7,6},{8,9},{9,8},{10,11... | collective-permute-start | bytes 294920 | tf_op jit(solution)/shard_map/ppermute | solution.py:38
  6.2 0.9 %collective-permute-done = bf16[4,32,384]{2,1,0:T(8,128)(2,1)S(1)} collective-permute-done((bf16[4,32,384]{2,1,0:T(8,128)(2,1)S(1)}, bf16[4,32,384]{2,1,0:T(8,128)(2,1)S(1)}, u32[]{:S(2)}, u32[]{:S(2)}) %collective-permute-start) | collective-permute-done | bytes 98336 | tf_op jit(solution)/shard_map/ppermute | solution.py:38
  7.2 1.3 %shard_map.85 = (bf16[16,32,384]{2,1,0:T(8,128)(2,1)S(1)}, bf16[16,32,384]{2,1,0:T(8,128)(2,1)S(1)}) custom-call(bf16[4,32,640]{2,1,0:T(8,128)(2,1)} %q_ref.1, bf16[4,32,640]{2,1,0:T(8,128)(2,1)} %keys_ref.3, bf16[4,32,640]{2,1,0:T(8,128)(2,1)} %values_ref.3, bf16[4,32,640]{2,1,0:T(8,128)(2,1)} %g_ref.1, bf16[4,32,384]{2,1,0:T(8,128)(2,1)S(1)} %add.6.after_ref), custom_call_target="tpu_custom_call" | custom-call | bytes 2097152 | tf_op jit(solution)/shard_map/pallas_call | solution.py:286
  8.5 0.4 %collective-permute-start.1 = (bf16[16,32,384]{2,1,0:T(8,128)(2,1)S(1)}, bf16[16,32,384]{2,1,0:T(8,128)(2,1)S(1)}, u32[]{:S(2)}, u32[]{:S(2)}) collective-permute-start(bf16[16,32,384]{2,1,0:T(8,128)(2,1)S(1)} %get-tuple-element.24), channel_id=1, source_target_pairs={{0,1},{1,0},{2,3},{3,2},{4,5},{5,4},{6,7},{7,6},{8,9},{9,8},{10,11... | collective-permute-start | bytes 1179656 | tf_op jit(solution)/shard_map/ppermute | solution.py:38
  8.9 0.0 collective-permute-start.2
  8.9 2.1 %collective-permute-start.4 = (bf16[2,32,384]{2,1,0:T(8,128)(2,1)S(1)}, bf16[2,32,384]{2,1,0:T(8,128)(2,1)S(1)}, u32[]{:S(2)}, u32[]{:S(2)}) collective-permute-start(bf16[2,32,384]{2,1,0:T(8,128)(2,1)S(1)} %slice_add_fusion), channel_id=1, source_target_pairs={{0,6},{1,7},{2,8},{3,9},{4,10},{5,11},{6,12},{7,13},{8,14},{9,15},... | collective-permute-start | bytes 147464 | tf_op jit(solution)/shard_map/ppermute | solution.py:33
  11.0 1.5 %collective-permute-start.3 = (bf16[2,32,384]{2,1,0:T(8,128)(2,1)S(1)}, bf16[2,32,384]{2,1,0:T(8,128)(2,1)S(1)}, u32[]{:S(2)}, u32[]{:S(2)}) collective-permute-start(bf16[2,32,384]{2,1,0:T(8,128)(2,1)S(1)} %slice_add_fusion), channel_id=1, source_target_pairs={{0,4},{1,5},{2,6},{3,7},{4,8},{5,9},{6,10},{7,11},{8,12},{9,13},{1... | collective-permute-start | bytes 147464 | tf_op jit(solution)/shard_map/ppermute | solution.py:33
  12.5 6.9 %collective-permute-done.4.r3 = bf16[2,32,384]{2,1,0:T(8,128)(2,1)S(1)} collective-permute-done((bf16[2,32,384]{2,1,0:T(8,128)(2,1)S(1)}, bf16[2,32,384]{2,1,0:T(8,128)(2,1)S(1)}, u32[]{:S(2)}, u32[]{:S(2)}) %collective-permute-start.4) | collective-permute-done | bytes 49184 | tf_op jit(solution)/shard_map/ppermute | solution.py:33
  19.5 2.6 %collective-permute-done.3.r2 = bf16[2,32,384]{2,1,0:T(8,128)(2,1)S(1)} collective-permute-done((bf16[2,32,384]{2,1,0:T(8,128)(2,1)S(1)}, bf16[2,32,384]{2,1,0:T(8,128)(2,1)S(1)}, u32[]{:S(2)}, u32[]{:S(2)}) %collective-permute-start.3) | collective-permute-done | bytes 49184 | tf_op jit(solution)/shard_map/ppermute | solution.py:33
  22.1 0.0 collective-permute-done.2.r1
  22.1 0.0 collective-permute-done.1.theirs_ref
  22.1 3.8 %shard_map.86 = (bf16[2,32,384]{2,1,0:T(8,128)(2,1)S(1)}, bf16[4,32,384]{2,1,0:T(8,128)(2,1)S(1)}) custom-call(s32[21]{0:T(128)S(1)} %get-tuple-element.20.meta_ref, bf16[16,32,384]{2,1,0:T(8,128)(2,1)S(1)} %get-tuple-element.23.mine_ref, bf16[16,32,384]{2,1,0:T(8,128)(2,1)S(1)} %collective-permute-done.1.theirs_ref, ...), custom_call_target="tpu_custom_call" | custom-call | flops 75497472 | bytes 2097152 | tf_op jit(solution)/shard_map/pallas_call | solution.py:286
  25.9 5.3 %shard_map.87 = (bf16[16,32,384]{2,1,0:T(8,128)(2,1)S(1)}, bf16[16,32,256]{2,1,0:T(8,128)(2,1)S(1)}, f32[4,32,384]{2,1,0:T(8,128)S(1)}) custom-call(s32[21]{0:T(128)S(1)} %get-tuple-element.20.meta_ref, bf16[16,32,384]{2,1,0:T(8,128)(2,1)S(1)} %get-tuple-element.23.mine_ref, bf16[16,32,384]{2,1,0:T(8,128)(2,1)S(1)} %collective-permute-done.1.theirs_ref, ...), custom_call_target="tpu_custom_call" | custom-call | flops 301989888 | bytes 4194304 | tf_op jit(solution)/shard_map/pallas_call | solution.py:286
  31.2 1.3 %collective-permute-start.5 = (bf16[16,32,256]{2,1,0:T(8,128)(2,1)S(1)}, bf16[16,32,256]{2,1,0:T(8,128)(2,1)S(1)}, u32[]{:S(2)}, u32[]{:S(2)}) collective-permute-start(bf16[16,32,256]{2,1,0:T(8,128)(2,1)S(1)} %get-tuple-element.27), channel_id=1, source_target_pairs={{0,1},{1,0},{2,3},{3,2},{4,5},{5,4},{6,7},{7,6},{8,9},{9,8},{10,11... | collective-permute-start | bytes 786440 | tf_op jit(solution)/shard_map/ppermute | solution.py:38
  32.5 1.0 %collective-permute-start.6 = (bf16[4,32,384]{2,1,0:T(8,128)(2,1)S(1)}, bf16[4,32,384]{2,1,0:T(8,128)(2,1)S(1)}, u32[]{:S(2)}, u32[]{:S(2)}) collective-permute-start(bf16[4,32,384]{2,1,0:T(8,128)(2,1)S(1)} %get-tuple-element.31), channel_id=1, source_target_pairs={{0,254},{1,255},{2,0},{3,1},{4,2},{5,3},{6,4},{7,5},{8,6},{9,7},{1... | collective-permute-start | bytes 294920 | tf_op jit(solution)/shard_map/ppermute | solution.py:33
  33.5 1.6 %collective-permute-start.8 = (bf16[2,32,384]{2,1,0:T(8,128)(2,1)S(1)}, bf16[2,32,384]{2,1,0:T(8,128)(2,1)S(1)}, u32[]{:S(2)}, u32[]{:S(2)}) collective-permute-start(bf16[2,32,384]{2,1,0:T(8,128)(2,1)S(1)} %get-tuple-element.25.after_ref), channel_id=1, source_target_pairs={{0,250},{1,251},{2,252},{3,253},{4,254},{5,255},{6,0},{7,1},{8,2},... | collective-permute-start | bytes 147464 | tf_op jit(solution)/shard_map/ppermute | solution.py:33
  35.1 2.0 %collective-permute-start.7 = (bf16[2,32,384]{2,1,0:T(8,128)(2,1)S(1)}, bf16[2,32,384]{2,1,0:T(8,128)(2,1)S(1)}, u32[]{:S(2)}, u32[]{:S(2)}) collective-permute-start(bf16[2,32,384]{2,1,0:T(8,128)(2,1)S(1)} %get-tuple-element.25.after_ref), channel_id=1, source_target_pairs={{0,252},{1,253},{2,254},{3,255},{4,0},{5,1},{6,2},{7,3},{8,4},{9,5... | collective-permute-start | bytes 147464 | tf_op jit(solution)/shard_map/ppermute | solution.py:33
  37.1 0.6 %collective-permute-done.8.r3 = bf16[2,32,384]{2,1,0:T(8,128)(2,1)S(1)} collective-permute-done((bf16[2,32,384]{2,1,0:T(8,128)(2,1)S(1)}, bf16[2,32,384]{2,1,0:T(8,128)(2,1)S(1)}, u32[]{:S(2)}, u32[]{:S(2)}) %collective-permute-start.8) | collective-permute-done | bytes 49184 | tf_op jit(solution)/shard_map/ppermute | solution.py:33
  37.7 1.9 %collective-permute-done.7.r2 = bf16[2,32,384]{2,1,0:T(8,128)(2,1)S(1)} collective-permute-done((bf16[2,32,384]{2,1,0:T(8,128)(2,1)S(1)}, bf16[2,32,384]{2,1,0:T(8,128)(2,1)S(1)}, u32[]{:S(2)}, u32[]{:S(2)}) %collective-permute-start.7) | collective-permute-done | bytes 49184 | tf_op jit(solution)/shard_map/ppermute | solution.py:33
  39.6 0.0 collective-permute-done.6.r1
  39.6 0.6 %shard_map.89 = (bf16[4,32,384]{2,1,0:T(8,128)(2,1)S(1)}, bf16[4,32,256]{2,1,0:T(8,128)(2,1)S(1)}) custom-call(s32[21]{0:T(128)S(1)} %get-tuple-element.20.meta_ref, f32[4,32,384]{2,1,0:T(8,128)S(1)} %get-tuple-element.30.touch_ref, bf16[4,32,384]{2,1,0:T(8,128)(2,1)S(1)} %collective-permute-done.6.r1, bf16[2,32,384]{2,1,0:T(8,128)(2,1)S(1)} %collective-permute-done.7.r2, ...), custom_call_target="tpu_custom_call" | custom-call | bytes 1048576 | tf_op jit(solution)/shard_map/pallas_call | solution.py:286
  40.2 1.9 %collective-permute-start.9 = (bf16[4,32,256]{2,1,0:T(8,128)(2,1)S(1)}, bf16[4,32,256]{2,1,0:T(8,128)(2,1)S(1)}, u32[]{:S(2)}, u32[]{:S(2)}) collective-permute-start(bf16[4,32,256]{2,1,0:T(8,128)(2,1)S(1)} %get-tuple-element.33), channel_id=1, source_target_pairs={{0,1},{1,0},{2,3},{3,2},{4,5},{5,4},{6,7},{7,6},{8,9},{9,8},{10,11... | collective-permute-start | bytes 196616 | tf_op jit(solution)/shard_map/ppermute | solution.py:38
  42.1 0.0 collective-permute-done.5.got_ref
  42.1 0.8 %shard_map.88 = (bf16[4,32,640]{2,1,0:T(8,128)(2,1)}, bf16[4,32,640]{2,1,0:T(8,128)(2,1)}) custom-call(bf16[16,32,384]{2,1,0:T(8,128)(2,1)S(1)} %get-tuple-element.26.keep_ref, bf16[16,32,256]{2,1,0:T(8,128)(2,1)S(1)} %collective-permute-done.5.got_ref), custom_call_target="tpu_custom_call" | custom-call | bytes 1048576 | tf_op jit(solution)/shard_map/pallas_call | solution.py:286
  42.8 0.1 collective-permute-done.9.touched_got_ref
  43.0 1.4 %shard_map.90 = (bf16[4,32,640]{2,1,0:T(8,128)(2,1)}, bf16[4,32,640]{2,1,0:T(8,128)(2,1)}) custom-call(s32[21]{0:T(128)S(1)} %get-tuple-element.20.meta_ref, bf16[16,32,384]{2,1,0:T(8,128)(2,1)S(1)} %get-tuple-element.26.keep_ref, bf16[16,32,256]{2,1,0:T(8,128)(2,1)S(1)} %collective-permute-done.5.got_ref, ...), custom_call_target="tpu_custom_call" | custom-call | bytes 1048576 | tf_op jit(solution)/shard_map/pallas_call | solution.py:286
  (2 shorter events, 0.0 us)
Async XLA Ops:
  0.6 0.7 %copy-start = (s32[128]{0:T(128)S(1)}, s32[128]{0:T(128)}, u32[]{:S(2)}) copy-start(s32[128]{0:T(128)} %param.9) | copy-start | bytes 1540
  2.9 4.2 %collective-permute-start = (bf16[4,32,384]{2,1,0:T(8,128)(2,1)S(1)}, bf16[4,32,384]{2,1,0:T(8,128)(2,1)S(1)}, u32[]{:S(2)}, u32[]{:S(2)}) collective-permute-start(bf16[4,32,384]{2,1,0:T(8,128)(2,1)S(1)} %get-tuple-element.22), channel_id=1, source_target_pairs={{0,1},{1,0},{2,3},{3,2},{4,5},{5,4},{6,7},{7,6},{8,9},{9,8},{10,11... | collective-permute-start | bytes 294920 | tf_op jit(solution)/shard_map/ppermute | solution.py:38
  8.5 13.6 %collective-permute-start.1 = (bf16[16,32,384]{2,1,0:T(8,128)(2,1)S(1)}, bf16[16,32,384]{2,1,0:T(8,128)(2,1)S(1)}, u32[]{:S(2)}, u32[]{:S(2)}) collective-permute-start(bf16[16,32,384]{2,1,0:T(8,128)(2,1)S(1)} %get-tuple-element.24), channel_id=1, source_target_pairs={{0,1},{1,0},{2,3},{3,2},{4,5},{5,4},{6,7},{7,6},{8,9},{9,8},{10,11... | collective-permute-start | bytes 1179656 | tf_op jit(solution)/shard_map/ppermute | solution.py:38
  8.9 13.2 %collective-permute-start.2 = (bf16[4,32,384]{2,1,0:T(8,128)(2,1)S(1)}, bf16[4,32,384]{2,1,0:T(8,128)(2,1)S(1)}, u32[]{:S(2)}, u32[]{:S(2)}) collective-permute-start(bf16[4,32,384]{2,1,0:T(8,128)(2,1)S(1)} %add.6.after_ref), channel_id=1, source_target_pairs={{0,2},{1,3},{2,4},{3,5},{4,6},{5,7},{6,8},{7,9},{8,10},{9,11},{10,... | collective-permute-start | bytes 294920 | tf_op jit(solution)/shard_map/ppermute | solution.py:33
  8.9 10.5 %collective-permute-start.4 = (bf16[2,32,384]{2,1,0:T(8,128)(2,1)S(1)}, bf16[2,32,384]{2,1,0:T(8,128)(2,1)S(1)}, u32[]{:S(2)}, u32[]{:S(2)}) collective-permute-start(bf16[2,32,384]{2,1,0:T(8,128)(2,1)S(1)} %slice_add_fusion), channel_id=1, source_target_pairs={{0,6},{1,7},{2,8},{3,9},{4,10},{5,11},{6,12},{7,13},{8,14},{9,15},... | collective-permute-start | bytes 147464 | tf_op jit(solution)/shard_map/ppermute | solution.py:33
  11.0 11.1 %collective-permute-start.3 = (bf16[2,32,384]{2,1,0:T(8,128)(2,1)S(1)}, bf16[2,32,384]{2,1,0:T(8,128)(2,1)S(1)}, u32[]{:S(2)}, u32[]{:S(2)}) collective-permute-start(bf16[2,32,384]{2,1,0:T(8,128)(2,1)S(1)} %slice_add_fusion), channel_id=1, source_target_pairs={{0,4},{1,5},{2,6},{3,7},{4,8},{5,9},{6,10},{7,11},{8,12},{9,13},{1... | collective-permute-start | bytes 147464 | tf_op jit(solution)/shard_map/ppermute | solution.py:33
  31.2 10.9 %collective-permute-start.5 = (bf16[16,32,256]{2,1,0:T(8,128)(2,1)S(1)}, bf16[16,32,256]{2,1,0:T(8,128)(2,1)S(1)}, u32[]{:S(2)}, u32[]{:S(2)}) collective-permute-start(bf16[16,32,256]{2,1,0:T(8,128)(2,1)S(1)} %get-tuple-element.27), channel_id=1, source_target_pairs={{0,1},{1,0},{2,3},{3,2},{4,5},{5,4},{6,7},{7,6},{8,9},{9,8},{10,11... | collective-permute-start | bytes 786440 | tf_op jit(solution)/shard_map/ppermute | solution.py:38
  32.5 7.1 %collective-permute-start.6 = (bf16[4,32,384]{2,1,0:T(8,128)(2,1)S(1)}, bf16[4,32,384]{2,1,0:T(8,128)(2,1)S(1)}, u32[]{:S(2)}, u32[]{:S(2)}) collective-permute-start(bf16[4,32,384]{2,1,0:T(8,128)(2,1)S(1)} %get-tuple-element.31), channel_id=1, source_target_pairs={{0,254},{1,255},{2,0},{3,1},{4,2},{5,3},{6,4},{7,5},{8,6},{9,7},{1... | collective-permute-start | bytes 294920 | tf_op jit(solution)/shard_map/ppermute | solution.py:33
  33.5 4.2 %collective-permute-start.8 = (bf16[2,32,384]{2,1,0:T(8,128)(2,1)S(1)}, bf16[2,32,384]{2,1,0:T(8,128)(2,1)S(1)}, u32[]{:S(2)}, u32[]{:S(2)}) collective-permute-start(bf16[2,32,384]{2,1,0:T(8,128)(2,1)S(1)} %get-tuple-element.25.after_ref), channel_id=1, source_target_pairs={{0,250},{1,251},{2,252},{3,253},{4,254},{5,255},{6,0},{7,1},{8,2},... | collective-permute-start | bytes 147464 | tf_op jit(solution)/shard_map/ppermute | solution.py:33
  35.1 4.4 %collective-permute-start.7 = (bf16[2,32,384]{2,1,0:T(8,128)(2,1)S(1)}, bf16[2,32,384]{2,1,0:T(8,128)(2,1)S(1)}, u32[]{:S(2)}, u32[]{:S(2)}) collective-permute-start(bf16[2,32,384]{2,1,0:T(8,128)(2,1)S(1)} %get-tuple-element.25.after_ref), channel_id=1, source_target_pairs={{0,252},{1,253},{2,254},{3,255},{4,0},{5,1},{6,2},{7,3},{8,4},{9,5... | collective-permute-start | bytes 147464 | tf_op jit(solution)/shard_map/ppermute | solution.py:33
  40.2 2.8 %collective-permute-start.9 = (bf16[4,32,256]{2,1,0:T(8,128)(2,1)S(1)}, bf16[4,32,256]{2,1,0:T(8,128)(2,1)S(1)}, u32[]{:S(2)}, u32[]{:S(2)}) collective-permute-start(bf16[4,32,256]{2,1,0:T(8,128)(2,1)S(1)} %get-tuple-element.33), channel_id=1, source_target_pairs={{0,1},{1,0},{2,3},{3,2},{4,5},{5,4},{6,7},{7,6},{8,9},{9,8},{10,11... | collective-permute-start | bytes 196616 | tf_op jit(solution)/shard_map/ppermute | solution.py:38
where the time goes:
time: 44.5 us; the launch traced here: 44.3 us
  starting transfers between devices  15.1 us (34%)
  Pallas kernels  14.7 us (33%)
  waiting for transfers between devices  13.1 us (29%)
  between operations  0.68 us (2%)
  local copies, waits for them, and re-layouts  0.65 us (1%)
    pallas_call x7, Pallas kernels, call(): pl.pallas_call(kernel, out_shape=outs, in_specs=in_specs, out_specs=out_s...  14.7 us
    ppermute x6, waiting for transfers between devices, ring(): lax.ppermute(value, 'tm', [(s, (s + steps) % count) for s in range(count)])  12 us
    ppermute x6, starting transfers between devices, ring(): lax.ppermute(value, 'tm', [(s, (s + steps) % count) for s in range(count)])  8.22 us
    ppermute x4, starting transfers between devices, swap(): return lax.ppermute(value, 'tm', [(s, s ^ 1) for s in range(count)])  6.91 us
    ppermute x4, waiting for transfers between devices, swap(): return lax.ppermute(value, 'tm', [(s, s ^ 1) for s in range(count)])  1.07 us
  transfers between devices with their start and end apart: 10, of which 6 were waited for; matrix products, arithmetic and copies ran while one was open for 0% of the time, Pallas kernels for 3%

commit v1 on v0

--- a/solution.py
+++ b/solution.py
@@ -47,7 +47,9 @@
     return pl.ds(pl.multiple_of(core * STEP, 128), SPAN)
 
 
-def prep_kernel(lengths_ref, keys_ref, values_ref, meta_ref, mine_ref, send_ref, frames, sems):
+def prep_kernel(clips_ref, keys_ref, values_ref, meta_ref, mine_ref, send_ref, lengths_ref, frames, sems):
+    count = pltpu.make_async_copy(clips_ref, lengths_ref, sems.at[2])
+    count.start()
     copies = [
         pltpu.make_async_copy(ref, frames.at[i], sems.at[i])
         for i, ref in enumerate((keys_ref, values_ref))
@@ -61,6 +63,7 @@
     rows = lax.broadcasted_iota(jnp.int32, (clips, clips), 0)
     columns = lax.broadcasted_iota(jnp.int32, (clips, clips), 1)
     earlier = jnp.where(rows < columns, 1.0, 0.0).astype(BF16)
+    count.wait()
     lengths = jnp.broadcast_to(lengths_ref[...].astype(F32), (16, clips)).astype(BF16)
     starts = jnp.dot(lengths, earlier, preferred_element_type=F32)[:1].astype(jnp.int32)
 
@@ -107,21 +110,19 @@
         copy.wait()
 
 
-def gather_slots(meta_ref, mine_ref, theirs_ref, received, q, keys, values, g):
-    core = place()[1]
-    for source, base in ((mine_ref, core * F), (theirs_ref, (1 - core) * F)):
-        for i, target in enumerate((q, keys, values, g)):
-            for j in range(F):
-                target[base + j] = source[i * F + j]
-    keys[HALO] = received[0][2]
-    values[HALO] = received[0][3]
-    back = meta_ref[BACK]
-    for k in range(1, REACH + 1):
-
-        @pl.when(back == k)
-        def _():
-            keys[REMOTE] = received[k - 1][0]
-            values[REMOTE] = received[k - 1][1]
+UNITS = C + C // 2
+UNIT = 4 * SIZE
+HALF = UNIT // 2
+
+
+def frames_of(unit):
+    return (unit,) if unit < C else (2 * (unit - C), 2 * (unit - C) + 1)
+
+
+def unit_of(load, unit):
+    if unit < C:
+        return load(unit, slice(0, UNIT))
+    return jnp.concatenate([load(i, slice(UNIT, SPAN)) for i in frames_of(unit)], axis=1)
 
 
 def spread(block):
@@ -136,86 +137,154 @@
 def fold(product):
     heads = product.shape[1] // SIZE
     tokens = product.shape[0] // heads
-    lane = lax.broadcasted_iota(jnp.int32, (tokens, product.shape[1]), 1)
-    result = product[:tokens]
-    for h in range(1, heads):
-        result = jnp.where(lane < h * SIZE, result, product[h * tokens : (h + 1) * tokens])
-    return result
+    lane = lax.broadcasted_iota(jnp.int32, (tokens, HALF), 1)
+    parts = []
+    for start in range(0, product.shape[1], HALF):
+        h = start // SIZE
+        columns = slice(start, start + HALF)
+        low = product[h * tokens : (h + 1) * tokens, columns]
+        high = product[(h + 1) * tokens : (h + 2) * tokens, columns]
+        parts.append(jnp.where(lane < SIZE, low, high))
+    return jnp.concatenate(parts, axis=1)
 
 
 def contract(a, b, da, db):
     return lax.dot_general(a, b, (((da,), (db,)), ((), ())), preferred_element_type=F32)
 
 
-def soft(keys, values, q, g):
-    scale = SIZE ** (-0.5)
-    scores = contract(keys, q, 1, 1) * scale
-    grad_prob = contract(values, g, 1, 1)
-    expos = jnp.exp(scores - jnp.max(scores, axis=0, keepdims=True))
-    prob = expos / jnp.sum(expos, axis=0, keepdims=True)
-    inner = jnp.sum(prob * grad_prob, axis=0, keepdims=True)
-    grad_score = prob * (grad_prob - inner) * scale
-    return prob.astype(BF16), grad_score.astype(BF16)
-
-
-GROUPS = tuple(
-    slice(start, min(start + 4 * SIZE, SPAN)) for start in range(0, SPAN, 4 * SIZE)
-)
-
-
-def pair(slots, own, prev, columns):
-    return jnp.concatenate([slots[own, :, columns], slots[prev, :, columns]], axis=0)
-
-
-def near_kernel(meta_ref, mine_ref, theirs_ref, r1, r2, r3, sums_ref, edge_ref, q, keys, values, g):
-    gather_slots(meta_ref, mine_ref, theirs_ref, (r1, r2, r3), q, keys, values, g)
-    tokens = q.shape[1]
-    for columns in GROUPS:
-        span = columns.stop - columns.start
-        key_total = jnp.zeros((tokens, span), F32)
-        value_total = jnp.zeros((tokens, span), F32)
+SCALE = SIZE ** (-0.5)
+
+
+def local_kernel(meta_ref, mine_ref, theirs_ref, qs, gs, own_k, own_v, prev_k, prev_v, s_prev, d_prev, slots):
+    core = place()[1]
+    for source, base in ((mine_ref, core * F), (theirs_ref, (1 - core) * F)):
+        for a in range(4):
+            for j in range(F):
+                slots[a, base + j] = source[a * F + j]
+    own = [jnp.minimum(meta_ref[OWN + i], C - 1) for i in range(C)]
+    prev = [jnp.minimum(meta_ref[PREV + i], C - 1) for i in range(C)]
+    for u in range(UNITS):
+        qs[u] = spread(unit_of(lambda i, columns: slots[0, i, :, columns], u))
+        gs[u] = spread(unit_of(lambda i, columns: slots[3, i, :, columns], u))
+        own_k[u] = unit_of(lambda i, columns: slots[1, own[i], :, columns], u)
+        own_v[u] = unit_of(lambda i, columns: slots[2, own[i], :, columns], u)
+        prev_k[u] = unit_of(lambda i, columns: slots[1, prev[i], :, columns], u)
+        prev_v[u] = unit_of(lambda i, columns: slots[2, prev[i], :, columns], u)
+    for u in range(UNITS):
+        s_prev[u] = contract(prev_k[u], qs[u], 1, 1) * SCALE
+        d_prev[u] = contract(prev_v[u], gs[u], 1, 1)
+
+
+def farther(meta_ref, r1, r2, r3, which):
+    back = meta_ref[BACK]
+    return jnp.where(back == 1, r1[which], jnp.where(back == 2, r2[which], r3[which]))
+
+
+def own_rows(meta_ref, local, far, u):
+    def load(i, columns):
+        here = local[u] if u < C else local[u, :, (i % 2) * HALF : (i % 2 + 1) * HALF]
+        return jnp.where(meta_ref[OWN + i] == REMOTE, far[:, columns], here)
+
+    return unit_of(load, u)
+
+
+def prev_rows(meta_ref, local, halo, u):
+    if u not in (0, C):
+        return local[u]
+    outside = meta_ref[PREV] == HALO
+    if u == 0:
+        return jnp.where(outside, halo[:, :UNIT], local[u])
+    left = jnp.where(outside, halo[:, UNIT:], local[u, :, :HALF])
+    return jnp.concatenate([left, local[u, :, HALF:]], axis=1)
+
+
+def near_kernel(
+    meta_ref, r1, r2, r3, qs, gs, own_k, own_v, prev_k, prev_v, s_prev, d_prev,
+    sums_ref, edge_ref, prob_ref, grad_ref, scores, grads,
+):
+    tokens = r1.shape[1]
+    far_k, far_v = farther(meta_ref, r1, r2, r3, 0), farther(meta_ref, r1, r2, r3, 1)
+    for u in range(UNITS):
+        scores[u, :tokens] = contract(own_rows(meta_ref, own_k, far_k, u), qs[u], 1, 1) * SCALE
+        grads[u, :tokens] = contract(own_rows(meta_ref, own_v, far_v, u), gs[u], 1, 1)
+        if u in (0, C):
+            scores[u, tokens:] = contract(prev_rows(meta_ref, prev_k, r1[2], u), qs[u], 1, 1) * SCALE
+            grads[u, tokens:] = contract(prev_rows(meta_ref, prev_v, r1[3], u), gs[u], 1, 1)
+        else:
+            scores[u, tokens:] = s_prev[u]
+            grads[u, tokens:] = d_prev[u]
+    for u in range(UNITS):
+        score, grad_prob = scores[u], grads[u]
+        expos = jnp.exp(score - jnp.max(score, axis=0, keepdims=True))
+        prob = expos * (1.0 / jnp.sum(expos, axis=0, keepdims=True))
+        inner = jnp.sum(prob * grad_prob, axis=0, keepdims=True)
+        prob_ref[u] = prob.astype(BF16)
+        grad_ref[u] = (prob * (grad_prob - inner) * SCALE).astype(BF16)
+    lane = lax.broadcasted_iota(jnp.int32, (tokens, UNIT // 2), 1)
+    width = UNIT // 2
+
+    def kept(ref, u):
+        flags = [meta_ref[OWN + i] == REMOTE for i in frames_of(u)]
+        block = ref[u, :tokens]
+        if u < C:
+            return jnp.where(flags[0], block, jnp.zeros_like(block))
+        inside = ((lane < SIZE) & flags[0]) | ((lane >= SIZE) & flags[1])
+        return jnp.where(inside, block, jnp.zeros_like(block))
+
+    halo = meta_ref[PREV] == HALO
+    for j, (ref, other) in enumerate(((grad_ref, qs), (prob_ref, gs))):
+        first = jnp.concatenate([kept(ref, u) for u in range(C)], axis=1)
+        total = contract(first, other[:C].reshape(C * width, UNIT), 1, 0).astype(BF16)
+        second = jnp.concatenate([kept(ref, u) for u in range(C, UNITS)], axis=1)
+        pairs = contract(second, other[C:].reshape((UNITS - C) * width, UNIT), 1, 0)
+        rest = (pairs[:, :HALF] + pairs[:, HALF:]).astype(BF16)
+        for target in (sums_ref, edge_ref):
+            target[j, :, :UNIT] = total
+            target[j, :, UNIT:] = rest
+        left = contract(ref[0, tokens:], other[0], 1, 0)
+        right = contract(ref[C, tokens:], other[C], 1, 0)[:, :HALF]
+        edge_ref[2 + j, :, :UNIT] = jnp.where(halo, left, 0.0).astype(BF16)
+        edge_ref[2 + j, :, UNIT:] = jnp.where(halo, right, 0.0).astype(BF16)
+
+
+def full_kernel(
+    meta_ref, r1, r2, r3, qs, gs, own_k, own_v, prev_k, prev_v, prob_ref, grad_ref,
+    keep_ref, send_ref, touch_ref, out, key_part, value_part, key_sum, value_sum,
+):
+    tokens = r1.shape[1]
+    far_k, far_v = farther(meta_ref, r1, r2, r3, 0), farther(meta_ref, r1, r2, r3, 1)
+
+    def place_unit(target, base, u, rows, block):
+        if u < C:
+            target[base + u, rows, :UNIT] = block
+        else:
+            for n, i in enumerate(frames_of(u)):
+                target[base + i, rows, UNIT:] = block[:, n * HALF : (n + 1) * HALF]
+
+    everything = slice(None)
+    for u in range(UNITS):
+        key = jnp.concatenate(
+            [own_rows(meta_ref, own_k, far_k, u), prev_rows(meta_ref, prev_k, r1[2], u)], axis=0
+        )
+        value = jnp.concatenate(
+            [own_rows(meta_ref, own_v, far_v, u), prev_rows(meta_ref, prev_v, r1[3], u)], axis=0
+        )
+        attended = fold(contract(prob_ref[u], value, 0, 0)).astype(BF16)
+        grad_q = fold(contract(grad_ref[u], key, 0, 0)).astype(BF16)
+        place_unit(out, 0, u, everything, attended)
+        place_unit(out, C, u, everything, grad_q)
+        place_unit(value_part, 0, u, everything, contract(prob_ref[u], gs[u], 1, 0))
+        place_unit(key_part, 0, u, everything, contract(grad_ref[u], qs[u], 1, 0))
+    for part, total in ((key_part, key_sum), (value_part, value_sum)):
         for i in range(C):
-            own, prev = meta_ref[OWN + i], meta_ref[PREV + i]
-            heads_q, heads_g = spread(q[i, :, columns]), spread(g[i, :, columns])
-            prob, grad_score = soft(
-                pair(keys, own, prev, columns), pair(values, own, prev, columns), heads_q, heads_g
-            )
-            rows = 2 * tokens if i == 0 else tokens
-            grad_value = contract(prob[:rows], heads_g, 1, 0)
-            grad_key = contract(grad_score[:rows], heads_q, 1, 0)
-            remote = own == REMOTE
-            key_total += jnp.where(remote, grad_key[:tokens], 0.0)
-            value_total += jnp.where(remote, grad_value[:tokens], 0.0)
-            if i == 0:
-                halo = prev == HALO
-                edge_ref[2, :, columns] = jnp.where(halo, grad_key[tokens:], 0.0).astype(BF16)
-                edge_ref[3, :, columns] = jnp.where(halo, grad_value[tokens:], 0.0).astype(BF16)
-        for target in (sums_ref, edge_ref):
-            target[0, :, columns] = key_total.astype(BF16)
-            target[1, :, columns] = value_total.astype(BF16)
-
-
-def full_kernel(meta_ref, mine_ref, theirs_ref, r1, r2, r3, after_ref, keep_ref, send_ref, touch_ref, *scratch):
-    q, keys, values, g, key_sum, value_sum, out = scratch
-    gather_slots(meta_ref, mine_ref, theirs_ref, (r1, r2, r3), q, keys, values, g)
-    key_sum[...] = jnp.zeros_like(key_sum)
-    value_sum[...] = jnp.zeros_like(value_sum)
-    tokens = q.shape[1]
+            here = jnp.where(meta_ref[PREV + i] == i, part[i, tokens:], 0.0)
+            if i + 1 < C:
+                here += jnp.where(meta_ref[PREV + i + 1] == i, part[i + 1, tokens:], 0.0)
+            total[i] = here
     for i in range(C):
-        own, prev = meta_ref[OWN + i], meta_ref[PREV + i]
-        for columns in GROUPS:
-            heads_q, heads_g = spread(q[i, :, columns]), spread(g[i, :, columns])
-            key = pair(keys, own, prev, columns)
-            value = pair(values, own, prev, columns)
-            prob, grad_score = soft(key, value, heads_q, heads_g)
-            out[i, :, columns] = fold(contract(prob, value, 0, 0)).astype(BF16)
-            out[C + i, :, columns] = fold(contract(grad_score, key, 0, 0)).astype(BF16)
-            grad_value = contract(prob, heads_g, 1, 0)
-            grad_key = contract(grad_score, heads_q, 1, 0)
-            key_sum[own, :, columns] += grad_key[:tokens]
-            value_sum[own, :, columns] += grad_value[:tokens]
-            key_sum[prev, :, columns] += grad_key[tokens:]
-            value_sum[prev, :, columns] += grad_value[tokens:]
+        own = meta_ref[OWN + i]
+        key_sum[own] += key_part[i, :tokens]
+        value_sum[own] += value_part[i, :tokens]
     for i in range(C):
         out[2 * C + i] = key_sum[i].astype(BF16)
         out[3 * C + i] = value_sum[i].astype(BF16)
@@ -308,11 +377,15 @@
 
     meta, own_edge, send_edge = call(
         prep_kernel,
-        (clip_lengths.reshape(1, -1), keys, values),
+        (pltpu.with_memory_space_constraint(clip_lengths.reshape(1, -1), pltpu.HBM), keys, values),
         (jax.ShapeDtypeStruct((META,), jnp.int32), shape(4, SPAN), shape(4, SPAN)),
-        [VMEM, HBM, HBM],
+        [HBM, HBM, HBM],
         (SMEM, VMEM, VMEM),
-        [pltpu.VMEM((2, F, tokens, WIDTH), BF16), pltpu.SemaphoreType.DMA((2,))],
+        [
+            pltpu.VMEM((1, clip_lengths.shape[0]), jnp.int32),
+            pltpu.VMEM((2, F, tokens, WIDTH), BF16),
+            pltpu.SemaphoreType.DMA((3,)),
+        ],
         size=1 << 20,
     )
     got_edge = swap(send_edge)
@@ -330,16 +403,27 @@
         size=2 << 20,
     )
     theirs = swap(send)
-    slots = [room(C), room(SLOTS), room(SLOTS), room(C)]
-    operands = (meta, mine, theirs, *received)
+    wide = jax.ShapeDtypeStruct((UNITS, UNIT // 2, UNIT), BF16)
+    rows = jax.ShapeDtypeStruct((UNITS, tokens, UNIT), BF16)
+    half = jax.ShapeDtypeStruct((UNITS, tokens, UNIT // 2), F32)
+    local = call(
+        local_kernel,
+        (meta, mine, theirs),
+        (wide, wide, rows, rows, rows, rows, half, half),
+        [SMEM] + [VMEM] * 2,
+        (VMEM,) * 8,
+        [pltpu.VMEM((4, C, tokens, SPAN), BF16)],
+        size=4 << 20,
+    )
+    soft = jax.ShapeDtypeStruct((UNITS, 2 * tokens, UNIT // 2), BF16)
     flops = 24 * C * tokens * tokens * SPAN
-    sums, edge_sums = call(
+    sums, edge_sums, prob, grad_score = call(
         near_kernel,
-        operands,
-        (shape(2, SPAN), shape(4, SPAN)),
-        [SMEM] + [VMEM] * 5,
-        (VMEM, VMEM),
-        slots,
+        (meta, *received, *local),
+        (shape(2, SPAN), shape(4, SPAN), soft, soft),
+        [SMEM] + [VMEM] * 11,
+        (VMEM,) * 4,
+        [pltpu.VMEM((UNITS, 2 * tokens, UNIT // 2), F32)] * 2,
         flops,
         2 << 20,
     )
@@ -347,11 +431,13 @@
     returned = (ring(edge_sums, -2), far[1], far[0])
     keep, send_out, touch = call(
         full_kernel,
-        (*operands, sums),
+        (meta, *received, *local[:6], prob, grad_score),
         (shape(4 * F, SPAN), shape(4 * F, REST), shape(4, SPAN, F32)),
-        [SMEM] + [VMEM] * 6,
+        [SMEM] + [VMEM] * 11,
         (VMEM,) * 3,
-        slots + [room(SLOTS, F32), room(SLOTS, F32), room(4 * C)],
+        [room(4 * C)]
+        + [pltpu.VMEM((C, 2 * tokens, SPAN), F32)] * 2
+        + [room(SLOTS, F32), room(SLOTS, F32)],
         4 * flops,
         4 << 20,
     )

time: 44.5 us -> 37.8 us (0.85)
  Pallas kernels: 14.7 us -> 9.93 us
  waiting for transfers between devices: 13.1 us -> 11.9 us
  local copies, waits for them, and re-layouts: 0.65 us -> 0 us
    pallas_call x7 -> x8, Pallas kernels: 14.7 us -> 9.93 us  [call(): pl.pallas_call(kernel, out_shape=outs, in_specs=in_specs, out_specs=out_s...]
    ppermute x6, waiting for transfers between devices: 12 us -> 10.8 us  [ring(): lax.ppermute(value, 'tm', [(s, (s + steps) % count) for s in range(count)])]
    unnamed x2 -> x0, local copies, waits for them, and re-layouts: 0.65 us -> none
  transfers between devices with their start and end apart: 10 -> 10, of which waited for: 6 -> 6; matrix products, arithmetic and copies ran while one was open for 0% -> 0% of each run, Pallas kernels for 3% -> 7%
where the time goes in v1:
time: 37.8 us; the launch traced here: 37.7 us
  starting transfers between devices  15.1 us (40%)
  waiting for transfers between devices  11.9 us (31%)
  Pallas kernels  9.93 us (26%)
  between operations  0.68 us (2%)
    ppermute x6, waiting for transfers between devices, ring(): lax.ppermute(value, 'tm', [(s, (s + steps) % count) for s in range(count)])  10.8 us
    pallas_call x8, Pallas kernels, call(): pl.pallas_call(kernel, out_shape=outs, in_specs=in_specs, out_specs=out_s...  9.93 us
    ppermute x6, starting transfers between devices, ring(): lax.ppermute(value, 'tm', [(s, (s + steps) % count) for s in range(count)])  8.23 us
    ppermute x4, starting transfers between devices, swap(): return lax.ppermute(value, 'tm', [(s, s ^ 1) for s in range(count)])  6.9 us
    ppermute x4, waiting for transfers between devices, swap(): return lax.ppermute(value, 'tm', [(s, s ^ 1) for s in range(count)])  1.07 us
  transfers between devices with their start and end apart: 10, of which 6 were waited for; matrix products, arithmetic and copies ran while one was open for 0% of the time, Pallas kernels for 7%

profile of v1, /device:TPU:1, one launch (start us, length us, event | category | flops | bytes accessed | tf_op | source)
XLA Modules:
  0.0 37.7 jit_solution(8208741475677695293)
XLA Ops:
  0.6 1.7 %shard_map.84 = (s32[21]{0:T(128)S(1)}, bf16[4,32,384]{2,1,0:T(8,128)(2,1)S(1)}, bf16[4,32,384]{2,1,0:T(8,128)(2,1)S(1)}) custom-call(s32[1,128]{1,0:T(1,128)} %bitcast.1, bf16[4,32,640]{2,1,0:T(8,128)(2,1)} %keys_ref.3, bf16[4,32,640]{2,1,0:T(8,128)(2,1)} %values_ref.3), custom_call_target="tpu_custom_call" | custom-call | bytes 1048576 | tf_op jit(solution)/shard_map/pallas_call | solution.py:355
  2.3 3.3 %collective-permute-start = (bf16[4,32,384]{2,1,0:T(8,128)(2,1)S(1)}, bf16[4,32,384]{2,1,0:T(8,128)(2,1)S(1)}, u32[]{:S(2)}, u32[]{:S(2)}) collective-permute-start(bf16[4,32,384]{2,1,0:T(8,128)(2,1)S(1)} %get-tuple-element.32), channel_id=1, source_target_pairs={{0,1},{1,0},{2,3},{3,2},{4,5},{5,4},{6,7},{7,6},{8,9},{9,8},{10,11... | collective-permute-start | bytes 294920 | tf_op jit(solution)/shard_map/ppermute | solution.py:38
  5.6 0.9 %collective-permute-done = bf16[4,32,384]{2,1,0:T(8,128)(2,1)S(1)} collective-permute-done((bf16[4,32,384]{2,1,0:T(8,128)(2,1)S(1)}, bf16[4,32,384]{2,1,0:T(8,128)(2,1)S(1)}, u32[]{:S(2)}, u32[]{:S(2)}) %collective-permute-start) | collective-permute-done | bytes 98336 | tf_op jit(solution)/shard_map/ppermute | solution.py:38
  6.6 1.3 %shard_map.85 = (bf16[16,32,384]{2,1,0:T(8,128)(2,1)S(1)}, bf16[16,32,384]{2,1,0:T(8,128)(2,1)S(1)}) custom-call(bf16[4,32,640]{2,1,0:T(8,128)(2,1)} %q_ref.1, bf16[4,32,640]{2,1,0:T(8,128)(2,1)} %keys_ref.3, bf16[4,32,640]{2,1,0:T(8,128)(2,1)} %values_ref.3, bf16[4,32,640]{2,1,0:T(8,128)(2,1)} %g_ref.1, bf16[4,32,384]{2,1,0:T(8,128)(2,1)S(1)} %add.6.after_ref), custom_call_target="tpu_custom_call" | custom-call | bytes 2097152 | tf_op jit(solution)/shard_map/pallas_call | solution.py:355
  7.9 0.4 %collective-permute-start.4 = (bf16[16,32,384]{2,1,0:T(8,128)(2,1)S(1)}, bf16[16,32,384]{2,1,0:T(8,128)(2,1)S(1)}, u32[]{:S(2)}, u32[]{:S(2)}) collective-permute-start(bf16[16,32,384]{2,1,0:T(8,128)(2,1)S(1)} %get-tuple-element.34), channel_id=1, source_target_pairs={{0,1},{1,0},{2,3},{3,2},{4,5},{5,4},{6,7},{7,6},{8,9},{9,8},{10,11... | collective-permute-start | bytes 1179656 | tf_op jit(solution)/shard_map/ppermute | solution.py:38
  8.3 0.0 collective-permute-start.1
  8.3 2.1 %collective-permute-start.3 = (bf16[2,32,384]{2,1,0:T(8,128)(2,1)S(1)}, bf16[2,32,384]{2,1,0:T(8,128)(2,1)S(1)}, u32[]{:S(2)}, u32[]{:S(2)}) collective-permute-start(bf16[2,32,384]{2,1,0:T(8,128)(2,1)S(1)} %slice_add_fusion), channel_id=1, source_target_pairs={{0,6},{1,7},{2,8},{3,9},{4,10},{5,11},{6,12},{7,13},{8,14},{9,15},... | collective-permute-start | bytes 147464 | tf_op jit(solution)/shard_map/ppermute | solution.py:33
  10.4 1.5 %collective-permute-start.2 = (bf16[2,32,384]{2,1,0:T(8,128)(2,1)S(1)}, bf16[2,32,384]{2,1,0:T(8,128)(2,1)S(1)}, u32[]{:S(2)}, u32[]{:S(2)}) collective-permute-start(bf16[2,32,384]{2,1,0:T(8,128)(2,1)S(1)} %slice_add_fusion), channel_id=1, source_target_pairs={{0,4},{1,5},{2,6},{3,7},{4,8},{5,9},{6,10},{7,11},{8,12},{9,13},{1... | collective-permute-start | bytes 147464 | tf_op jit(solution)/shard_map/ppermute | solution.py:33
  11.9 0.0 collective-permute-done.4.theirs_ref
  11.9 1.2 %shard_map.86 = (bf16[12,128,256]{2,1,0:T(8,128)(2,1)S(1)}, bf16[12,128,256]{2,1,0:T(8,128)(2,1)S(1)}, bf16[12,32,256]{2,1,0:T(8,128)(2,1)S(1)}, bf16[12,32,256]...) custom-call(s32[21]{0:T(128)S(1)} %get-tuple-element.30.meta_ref, ...), custom_call_target="tpu_custom_call" | custom-call | bytes 4194304 | tf_op jit(solution)/shard_map/pallas_call | solution.py:355
  13.1 5.8 %collective-permute-done.3.r3 = bf16[2,32,384]{2,1,0:T(8,128)(2,1)S(1)} collective-permute-done((bf16[2,32,384]{2,1,0:T(8,128)(2,1)S(1)}, bf16[2,32,384]{2,1,0:T(8,128)(2,1)S(1)}, u32[]{:S(2)}, u32[]{:S(2)}) %collective-permute-start.3) | collective-permute-done | bytes 49184 | tf_op jit(solution)/shard_map/ppermute | solution.py:33
  18.8 2.6 %collective-permute-done.2.r2 = bf16[2,32,384]{2,1,0:T(8,128)(2,1)S(1)} collective-permute-done((bf16[2,32,384]{2,1,0:T(8,128)(2,1)S(1)}, bf16[2,32,384]{2,1,0:T(8,128)(2,1)S(1)}, u32[]{:S(2)}, u32[]{:S(2)}) %collective-permute-start.2) | collective-permute-done | bytes 49184 | tf_op jit(solution)/shard_map/ppermute | solution.py:33
  21.4 0.0 collective-permute-done.1.r1
  21.5 1.6 %shard_map.87 = (bf16[2,32,384]{2,1,0:T(8,128)(2,1)S(1)}, bf16[4,32,384]{2,1,0:T(8,128)(2,1)S(1)}, bf16[12,64,128]{2,1,0:T(8,128)(2,1)S(1)}, bf16[12,64,128]{2,1,0:T(8,128)(2,1)S(1)}) custom-call(s32[21]{0:T(128)S(1)} %get-tuple-element.30.meta_ref, bf16[4,32,384]{2,1,0:T(8,128)(2,1)S(1)} %collective-permute-done.1.r1, ...), custom_call_target="tpu_custom_call" | custom-call | flops 75497472 | bytes 2097152 | tf_op jit(solution)/shard_map/pallas_call | solution.py:355
  23.0 1.5 %shard_map.88 = (bf16[16,32,384]{2,1,0:T(8,128)(2,1)S(1)}, bf16[16,32,256]{2,1,0:T(8,128)(2,1)S(1)}, f32[4,32,384]{2,1,0:T(8,128)S(1)}) custom-call(s32[21]{0:T(128)S(1)} %get-tuple-element.30.meta_ref, bf16[4,32,384]{2,1,0:T(8,128)(2,1)S(1)} %collective-permute-done.1.r1, bf16[2,32,384]{2,1,0:T(8,128)(2,1)S(1)} %collective-permute-done.2.r2, ...), custom_call_target="tpu_custom_call" | custom-call | flops 301989888 | bytes 4194304 | tf_op jit(solution)/shard_map/pallas_call | solution.py:355
  24.6 1.3 %collective-permute-start.5 = (bf16[16,32,256]{2,1,0:T(8,128)(2,1)S(1)}, bf16[16,32,256]{2,1,0:T(8,128)(2,1)S(1)}, u32[]{:S(2)}, u32[]{:S(2)}) collective-permute-start(bf16[16,32,256]{2,1,0:T(8,128)(2,1)S(1)} %get-tuple-element.46), channel_id=1, source_target_pairs={{0,1},{1,0},{2,3},{3,2},{4,5},{5,4},{6,7},{7,6},{8,9},{9,8},{10,11... | collective-permute-start | bytes 786440 | tf_op jit(solution)/shard_map/ppermute | solution.py:38
  25.8 1.0 %collective-permute-start.6 = (bf16[4,32,384]{2,1,0:T(8,128)(2,1)S(1)}, bf16[4,32,384]{2,1,0:T(8,128)(2,1)S(1)}, u32[]{:S(2)}, u32[]{:S(2)}) collective-permute-start(bf16[4,32,384]{2,1,0:T(8,128)(2,1)S(1)} %get-tuple-element.50), channel_id=1, source_target_pairs={{0,254},{1,255},{2,0},{3,1},{4,2},{5,3},{6,4},{7,5},{8,6},{9,7},{1... | collective-permute-start | bytes 294920 | tf_op jit(solution)/shard_map/ppermute | solution.py:33
  26.9 1.6 %collective-permute-start.8 = (bf16[2,32,384]{2,1,0:T(8,128)(2,1)S(1)}, bf16[2,32,384]{2,1,0:T(8,128)(2,1)S(1)}, u32[]{:S(2)}, u32[]{:S(2)}) collective-permute-start(bf16[2,32,384]{2,1,0:T(8,128)(2,1)S(1)} %get-tuple-element.51), channel_id=1, source_target_pairs={{0,250},{1,251},{2,252},{3,253},{4,254},{5,255},{6,0},{7,1},{8,2},... | collective-permute-start | bytes 147464 | tf_op jit(solution)/shard_map/ppermute | solution.py:33
  28.5 2.0 %collective-permute-start.7 = (bf16[2,32,384]{2,1,0:T(8,128)(2,1)S(1)}, bf16[2,32,384]{2,1,0:T(8,128)(2,1)S(1)}, u32[]{:S(2)}, u32[]{:S(2)}) collective-permute-start(bf16[2,32,384]{2,1,0:T(8,128)(2,1)S(1)} %get-tuple-element.51), channel_id=1, source_target_pairs={{0,252},{1,253},{2,254},{3,255},{4,0},{5,1},{6,2},{7,3},{8,4},{9,5... | collective-permute-start | bytes 147464 | tf_op jit(solution)/shard_map/ppermute | solution.py:33
  30.5 0.6 %collective-permute-done.8.r3 = bf16[2,32,384]{2,1,0:T(8,128)(2,1)S(1)} collective-permute-done((bf16[2,32,384]{2,1,0:T(8,128)(2,1)S(1)}, bf16[2,32,384]{2,1,0:T(8,128)(2,1)S(1)}, u32[]{:S(2)}, u32[]{:S(2)}) %collective-permute-start.8) | collective-permute-done | bytes 49184 | tf_op jit(solution)/shard_map/ppermute | solution.py:33
  31.0 1.9 %collective-permute-done.7.r2 = bf16[2,32,384]{2,1,0:T(8,128)(2,1)S(1)} collective-permute-done((bf16[2,32,384]{2,1,0:T(8,128)(2,1)S(1)}, bf16[2,32,384]{2,1,0:T(8,128)(2,1)S(1)}, u32[]{:S(2)}, u32[]{:S(2)}) %collective-permute-start.7) | collective-permute-done | bytes 49184 | tf_op jit(solution)/shard_map/ppermute | solution.py:33
  32.9 0.0 collective-permute-done.6.r1
  32.9 0.6 %shard_map.90 = (bf16[4,32,384]{2,1,0:T(8,128)(2,1)S(1)}, bf16[4,32,256]{2,1,0:T(8,128)(2,1)S(1)}) custom-call(s32[21]{0:T(128)S(1)} %get-tuple-element.30.meta_ref, f32[4,32,384]{2,1,0:T(8,128)S(1)} %get-tuple-element.49.touch_ref, bf16[4,32,384]{2,1,0:T(8,128)(2,1)S(1)} %collective-permute-done.6.r1, bf16[2,32,384]{2,1,0:T(8,128)(2,1)S(1)} %collective-permute-done.7.r2, ...), custom_call_target="tpu_custom_call" | custom-call | bytes 1048576 | tf_op jit(solution)/shard_map/pallas_call | solution.py:355
  33.5 1.9 %collective-permute-start.9 = (bf16[4,32,256]{2,1,0:T(8,128)(2,1)S(1)}, bf16[4,32,256]{2,1,0:T(8,128)(2,1)S(1)}, u32[]{:S(2)}, u32[]{:S(2)}) collective-permute-start(bf16[4,32,256]{2,1,0:T(8,128)(2,1)S(1)} %get-tuple-element.53), channel_id=1, source_target_pairs={{0,1},{1,0},{2,3},{3,2},{4,5},{5,4},{6,7},{7,6},{8,9},{9,8},{10,11... | collective-permute-start | bytes 196616 | tf_op jit(solution)/shard_map/ppermute | solution.py:38
  35.4 0.0 collective-permute-done.5.got_ref
  35.4 0.8 %shard_map.89 = (bf16[4,32,640]{2,1,0:T(8,128)(2,1)}, bf16[4,32,640]{2,1,0:T(8,128)(2,1)}) custom-call(bf16[16,32,384]{2,1,0:T(8,128)(2,1)S(1)} %get-tuple-element.45.keep_ref, bf16[16,32,256]{2,1,0:T(8,128)(2,1)S(1)} %collective-permute-done.5.got_ref), custom_call_target="tpu_custom_call" | custom-call | bytes 1048576 | tf_op jit(solution)/shard_map/pallas_call | solution.py:355
  36.2 0.1 collective-permute-done.9.touched_got_ref
  36.3 1.4 %shard_map.91 = (bf16[4,32,640]{2,1,0:T(8,128)(2,1)}, bf16[4,32,640]{2,1,0:T(8,128)(2,1)}) custom-call(s32[21]{0:T(128)S(1)} %get-tuple-element.30.meta_ref, bf16[16,32,384]{2,1,0:T(8,128)(2,1)S(1)} %get-tuple-element.45.keep_ref, bf16[16,32,256]{2,1,0:T(8,128)(2,1)S(1)} %collective-permute-done.5.got_ref, ...), custom_call_target="tpu_custom_call" | custom-call | bytes 1048576 | tf_op jit(solution)/shard_map/pallas_call | solution.py:355
  (2 shorter events, 0.0 us)
Async XLA Ops:
  2.3 4.2 %collective-permute-start = (bf16[4,32,384]{2,1,0:T(8,128)(2,1)S(1)}, bf16[4,32,384]{2,1,0:T(8,128)(2,1)S(1)}, u32[]{:S(2)}, u32[]{:S(2)}) collective-permute-start(bf16[4,32,384]{2,1,0:T(8,128)(2,1)S(1)} %get-tuple-element.32), channel_id=1, source_target_pairs={{0,1},{1,0},{2,3},{3,2},{4,5},{5,4},{6,7},{7,6},{8,9},{9,8},{10,11... | collective-permute-start | bytes 294920 | tf_op jit(solution)/shard_map/ppermute | solution.py:38
  7.9 4.1 %collective-permute-start.4 = (bf16[16,32,384]{2,1,0:T(8,128)(2,1)S(1)}, bf16[16,32,384]{2,1,0:T(8,128)(2,1)S(1)}, u32[]{:S(2)}, u32[]{:S(2)}) collective-permute-start(bf16[16,32,384]{2,1,0:T(8,128)(2,1)S(1)} %get-tuple-element.34), channel_id=1, source_target_pairs={{0,1},{1,0},{2,3},{3,2},{4,5},{5,4},{6,7},{7,6},{8,9},{9,8},{10,11... | collective-permute-start | bytes 1179656 | tf_op jit(solution)/shard_map/ppermute | solution.py:38
  8.3 13.2 %collective-permute-start.1 = (bf16[4,32,384]{2,1,0:T(8,128)(2,1)S(1)}, bf16[4,32,384]{2,1,0:T(8,128)(2,1)S(1)}, u32[]{:S(2)}, u32[]{:S(2)}) collective-permute-start(bf16[4,32,384]{2,1,0:T(8,128)(2,1)S(1)} %add.6.after_ref), channel_id=1, source_target_pairs={{0,2},{1,3},{2,4},{3,5},{4,6},{5,7},{6,8},{7,9},{8,10},{9,11},{10,... | collective-permute-start | bytes 294920 | tf_op jit(solution)/shard_map/ppermute | solution.py:33
  8.3 10.5 %collective-permute-start.3 = (bf16[2,32,384]{2,1,0:T(8,128)(2,1)S(1)}, bf16[2,32,384]{2,1,0:T(8,128)(2,1)S(1)}, u32[]{:S(2)}, u32[]{:S(2)}) collective-permute-start(bf16[2,32,384]{2,1,0:T(8,128)(2,1)S(1)} %slice_add_fusion), channel_id=1, source_target_pairs={{0,6},{1,7},{2,8},{3,9},{4,10},{5,11},{6,12},{7,13},{8,14},{9,15},... | collective-permute-start | bytes 147464 | tf_op jit(solution)/shard_map/ppermute | solution.py:33
  10.4 11.1 %collective-permute-start.2 = (bf16[2,32,384]{2,1,0:T(8,128)(2,1)S(1)}, bf16[2,32,384]{2,1,0:T(8,128)(2,1)S(1)}, u32[]{:S(2)}, u32[]{:S(2)}) collective-permute-start(bf16[2,32,384]{2,1,0:T(8,128)(2,1)S(1)} %slice_add_fusion), channel_id=1, source_target_pairs={{0,4},{1,5},{2,6},{3,7},{4,8},{5,9},{6,10},{7,11},{8,12},{9,13},{1... | collective-permute-start | bytes 147464 | tf_op jit(solution)/shard_map/ppermute | solution.py:33
  24.6 10.9 %collective-permute-start.5 = (bf16[16,32,256]{2,1,0:T(8,128)(2,1)S(1)}, bf16[16,32,256]{2,1,0:T(8,128)(2,1)S(1)}, u32[]{:S(2)}, u32[]{:S(2)}) collective-permute-start(bf16[16,32,256]{2,1,0:T(8,128)(2,1)S(1)} %get-tuple-element.46), channel_id=1, source_target_pairs={{0,1},{1,0},{2,3},{3,2},{4,5},{5,4},{6,7},{7,6},{8,9},{9,8},{10,11... | collective-permute-start | bytes 786440 | tf_op jit(solution)/shard_map/ppermute | solution.py:38
  25.8 7.1 %collective-permute-start.6 = (bf16[4,32,384]{2,1,0:T(8,128)(2,1)S(1)}, bf16[4,32,384]{2,1,0:T(8,128)(2,1)S(1)}, u32[]{:S(2)}, u32[]{:S(2)}) collective-permute-start(bf16[4,32,384]{2,1,0:T(8,128)(2,1)S(1)} %get-tuple-element.50), channel_id=1, source_target_pairs={{0,254},{1,255},{2,0},{3,1},{4,2},{5,3},{6,4},{7,5},{8,6},{9,7},{1... | collective-permute-start | bytes 294920 | tf_op jit(solution)/shard_map/ppermute | solution.py:33
  26.9 4.2 %collective-permute-start.8 = (bf16[2,32,384]{2,1,0:T(8,128)(2,1)S(1)}, bf16[2,32,384]{2,1,0:T(8,128)(2,1)S(1)}, u32[]{:S(2)}, u32[]{:S(2)}) collective-permute-start(bf16[2,32,384]{2,1,0:T(8,128)(2,1)S(1)} %get-tuple-element.51), channel_id=1, source_target_pairs={{0,250},{1,251},{2,252},{3,253},{4,254},{5,255},{6,0},{7,1},{8,2},... | collective-permute-start | bytes 147464 | tf_op jit(solution)/shard_map/ppermute | solution.py:33
  28.5 4.4 %collective-permute-start.7 = (bf16[2,32,384]{2,1,0:T(8,128)(2,1)S(1)}, bf16[2,32,384]{2,1,0:T(8,128)(2,1)S(1)}, u32[]{:S(2)}, u32[]{:S(2)}) collective-permute-start(bf16[2,32,384]{2,1,0:T(8,128)(2,1)S(1)} %get-tuple-element.51), channel_id=1, source_target_pairs={{0,252},{1,253},{2,254},{3,255},{4,0},{5,1},{6,2},{7,3},{8,4},{9,5... | collective-permute-start | bytes 147464 | tf_op jit(solution)/shard_map/ppermute | solution.py:33
  33.5 2.8 %collective-permute-start.9 = (bf16[4,32,256]{2,1,0:T(8,128)(2,1)S(1)}, bf16[4,32,256]{2,1,0:T(8,128)(2,1)S(1)}, u32[]{:S(2)}, u32[]{:S(2)}) collective-permute-start(bf16[4,32,256]{2,1,0:T(8,128)(2,1)S(1)} %get-tuple-element.53), channel_id=1, source_target_pairs={{0,1},{1,0},{2,3},{3,2},{4,5},{5,4},{6,7},{7,6},{8,9},{9,8},{10,11... | collective-permute-start | bytes 196616 | tf_op jit(solution)/shard_map/ppermute | solution.py:38

commit v2 on v1

--- a/solution.py
+++ b/solution.py
@@ -155,7 +155,12 @@
 SCALE = SIZE ** (-0.5)
 
 
-def local_kernel(meta_ref, mine_ref, theirs_ref, qs, gs, own_k, own_v, prev_k, prev_v, s_prev, d_prev, slots):
+EDGES = (0, C)
+
+
+def local_kernel(
+    meta_ref, mine_ref, theirs_ref, qs, gs, own_k, own_v, prev_k, prev_v, e_prev, d_prev, stats, qt, gt, slots
+):
     core = place()[1]
     for source, base in ((mine_ref, core * F), (theirs_ref, (1 - core) * F)):
         for a in range(4):
@@ -164,15 +169,26 @@
     own = [jnp.minimum(meta_ref[OWN + i], C - 1) for i in range(C)]
     prev = [jnp.minimum(meta_ref[PREV + i], C - 1) for i in range(C)]
     for u in range(UNITS):
-        qs[u] = spread(unit_of(lambda i, columns: slots[0, i, :, columns], u))
-        gs[u] = spread(unit_of(lambda i, columns: slots[3, i, :, columns], u))
+        q = spread(unit_of(lambda i, columns: slots[0, i, :, columns], u) * jnp.asarray(SCALE, BF16))
+        g = spread(unit_of(lambda i, columns: slots[3, i, :, columns], u))
+        qs[u], gs[u] = q, g
+        qt[u], gt[u] = q.T, g.T
         own_k[u] = unit_of(lambda i, columns: slots[1, own[i], :, columns], u)
         own_v[u] = unit_of(lambda i, columns: slots[2, own[i], :, columns], u)
         prev_k[u] = unit_of(lambda i, columns: slots[1, prev[i], :, columns], u)
         prev_v[u] = unit_of(lambda i, columns: slots[2, prev[i], :, columns], u)
     for u in range(UNITS):
-        s_prev[u] = contract(prev_k[u], qs[u], 1, 1) * SCALE
-        d_prev[u] = contract(prev_v[u], gs[u], 1, 1)
+        if u in EDGES:
+            continue
+        scores = contract(prev_k[u], qt[u], 1, 0)
+        grad_prob = contract(prev_v[u], gt[u], 1, 0)
+        top = jnp.max(scores, axis=0, keepdims=True)
+        expos = jnp.exp(scores - top)
+        e_prev[u] = expos
+        d_prev[u] = grad_prob
+        stats[u, 0:1] = top
+        stats[u, 1:2] = jnp.sum(expos, axis=0, keepdims=True)
+        stats[u, 2:3] = jnp.sum(expos * grad_prob, axis=0, keepdims=True)
 
 
 def farther(meta_ref, r1, r2, r3, which):
@@ -199,57 +215,87 @@
 
 
 def near_kernel(
-    meta_ref, r1, r2, r3, qs, gs, own_k, own_v, prev_k, prev_v, s_prev, d_prev,
-    sums_ref, edge_ref, prob_ref, grad_ref, scores, grads,
+    meta_ref, r1, r2, r3, qs, gs, own_k, own_v, prev_k, prev_v, stats, qt, gt,
+    sums_ref, edge_ref, prob_ref, grad_ref, first_ref, merged_ref,
 ):
     tokens = r1.shape[1]
     far_k, far_v = farther(meta_ref, r1, r2, r3, 0), farther(meta_ref, r1, r2, r3, 1)
-    for u in range(UNITS):
-        scores[u, :tokens] = contract(own_rows(meta_ref, own_k, far_k, u), qs[u], 1, 1) * SCALE
-        grads[u, :tokens] = contract(own_rows(meta_ref, own_v, far_v, u), gs[u], 1, 1)
-        if u in (0, C):
-            scores[u, tokens:] = contract(prev_rows(meta_ref, prev_k, r1[2], u), qs[u], 1, 1) * SCALE
-            grads[u, tokens:] = contract(prev_rows(meta_ref, prev_v, r1[3], u), gs[u], 1, 1)
-        else:
-            scores[u, tokens:] = s_prev[u]
-            grads[u, tokens:] = d_prev[u]
-    for u in range(UNITS):
-        score, grad_prob = scores[u], grads[u]
-        expos = jnp.exp(score - jnp.max(score, axis=0, keepdims=True))
-        prob = expos * (1.0 / jnp.sum(expos, axis=0, keepdims=True))
-        inner = jnp.sum(prob * grad_prob, axis=0, keepdims=True)
-        prob_ref[u] = prob.astype(BF16)
-        grad_ref[u] = (prob * (grad_prob - inner) * SCALE).astype(BF16)
     lane = lax.broadcasted_iota(jnp.int32, (tokens, UNIT // 2), 1)
-    width = UNIT // 2
-
-    def kept(ref, u):
+
+    def total(block):
+        return jnp.sum(block, axis=0, keepdims=True)
+
+    def kept(block, u):
         flags = [meta_ref[OWN + i] == REMOTE for i in frames_of(u)]
-        block = ref[u, :tokens]
         if u < C:
             return jnp.where(flags[0], block, jnp.zeros_like(block))
         inside = ((lane < SIZE) & flags[0]) | ((lane >= SIZE) & flags[1])
         return jnp.where(inside, block, jnp.zeros_like(block))
 
+    def products(u):
+        score = contract(own_rows(meta_ref, own_k, far_k, u), qt[u], 1, 0)
+        grad_prob = contract(own_rows(meta_ref, own_v, far_v, u), gt[u], 1, 0)
+        if u not in EDGES:
+            return score, grad_prob
+        before = contract(prev_rows(meta_ref, prev_k, r1[2], u), qt[u], 1, 0)
+        grad_before = contract(prev_rows(meta_ref, prev_v, r1[3], u), gt[u], 1, 0)
+        return score, grad_prob, before, grad_before
+
+    def softened(u, score, grad_prob, before=None, grad_before=None):
+        top = jnp.max(score, axis=0, keepdims=True)
+        if u in EDGES:
+            n = EDGES.index(u)
+            top = jnp.maximum(top, jnp.max(before, axis=0, keepdims=True))
+            expos, earlier = jnp.exp(score - top), jnp.exp(before - top)
+            inverse = 1.0 / (total(expos) + total(earlier))
+            inner = (total(expos * grad_prob) + total(earlier * grad_before)) * inverse
+            prob = earlier * inverse
+            first_ref[n, 0] = prob.astype(BF16)
+            first_ref[n, 1] = (prob * (grad_before - inner)).astype(BF16)
+        else:
+            older = stats[u, 0:1]
+            top = jnp.maximum(top, older)
+            expos, rescale = jnp.exp(score - top), jnp.exp(older - top)
+            inverse = 1.0 / (total(expos) + rescale * stats[u, 1:2])
+            inner = (total(expos * grad_prob) + rescale * stats[u, 2:3]) * inverse
+            merged_ref[u, 0:1] = rescale * inverse
+            merged_ref[u, 1:2] = inner
+        prob = expos * inverse
+        low = prob.astype(BF16)
+        low_grad = (prob * (grad_prob - inner)).astype(BF16)
+        prob_ref[u] = low
+        grad_ref[u] = low_grad
+        return kept(low_grad, u), kept(low, u)
+
     halo = meta_ref[PREV] == HALO
-    for j, (ref, other) in enumerate(((grad_ref, qs), (prob_ref, gs))):
-        first = jnp.concatenate([kept(ref, u) for u in range(C)], axis=1)
-        total = contract(first, other[:C].reshape(C * width, UNIT), 1, 0).astype(BF16)
-        second = jnp.concatenate([kept(ref, u) for u in range(C, UNITS)], axis=1)
-        pairs = contract(second, other[C:].reshape((UNITS - C) * width, UNIT), 1, 0)
+    sums = [[None, None], [None, None]]
+    ahead = 12
+    ready = {u: products(u) for u in range(ahead)}
+    for u in range(0, UNITS, 2):
+        soft = [softened(v, *ready.pop(v)) for v in (u, u + 1)]
+        for v in range(u + ahead, min(u + ahead + 2, UNITS)):
+            ready[v] = products(v)
+        part = int(u >= C)
+        for j, other in enumerate((qs, gs)):
+            left = jnp.concatenate([soft[0][j], soft[1][j]], axis=1)
+            right = other[u : u + 2].reshape(UNIT, UNIT)
+            product = contract(left, right, 1, 0)
+            sums[j][part] = product if sums[j][part] is None else sums[j][part] + product
+    for j, other in enumerate((qs, gs)):
+        pairs = sums[j][1]
         rest = (pairs[:, :HALF] + pairs[:, HALF:]).astype(BF16)
         for target in (sums_ref, edge_ref):
-            target[j, :, :UNIT] = total
+            target[j, :, :UNIT] = sums[j][0].astype(BF16)
             target[j, :, UNIT:] = rest
-        left = contract(ref[0, tokens:], other[0], 1, 0)
-        right = contract(ref[C, tokens:], other[C], 1, 0)[:, :HALF]
+        left = contract(first_ref[0, 1 - j], other[0], 1, 0)
+        right = contract(first_ref[1, 1 - j], other[C], 1, 0)[:, :HALF]
         edge_ref[2 + j, :, :UNIT] = jnp.where(halo, left, 0.0).astype(BF16)
         edge_ref[2 + j, :, UNIT:] = jnp.where(halo, right, 0.0).astype(BF16)
 
 
 def full_kernel(
-    meta_ref, r1, r2, r3, qs, gs, own_k, own_v, prev_k, prev_v, prob_ref, grad_ref,
-    keep_ref, send_ref, touch_ref, out, key_part, value_part, key_sum, value_sum,
+    meta_ref, r1, r2, r3, qs, gs, own_k, own_v, prev_k, prev_v, e_prev, d_prev,
+    prob_ref, grad_ref, first_ref, merged_ref, keep_ref, send_ref, touch_ref, out, key_part, value_part, key_sum, value_sum,
 ):
     tokens = r1.shape[1]
     far_k, far_v = farther(meta_ref, r1, r2, r3, 0), farther(meta_ref, r1, r2, r3, 1)
@@ -269,12 +315,21 @@
         value = jnp.concatenate(
             [own_rows(meta_ref, own_v, far_v, u), prev_rows(meta_ref, prev_v, r1[3], u)], axis=0
         )
-        attended = fold(contract(prob_ref[u], value, 0, 0)).astype(BF16)
-        grad_q = fold(contract(grad_ref[u], key, 0, 0)).astype(BF16)
+        if u in EDGES:
+            n = EDGES.index(u)
+            before, grad_before = first_ref[n, 0], first_ref[n, 1]
+        else:
+            wide = e_prev[u] * merged_ref[u, 0:1]
+            before = wide.astype(BF16)
+            grad_before = (wide * (d_prev[u] - merged_ref[u, 1:2])).astype(BF16)
+        prob = jnp.concatenate([prob_ref[u], before], axis=0)
+        grad = jnp.concatenate([grad_ref[u], grad_before], axis=0)
+        attended = fold(contract(prob, value, 0, 0)).astype(BF16)
+        grad_q = (fold(contract(grad, key, 0, 0)) * SCALE).astype(BF16)
         place_unit(out, 0, u, everything, attended)
         place_unit(out, C, u, everything, grad_q)
-        place_unit(value_part, 0, u, everything, contract(prob_ref[u], gs[u], 1, 0))
-        place_unit(key_part, 0, u, everything, contract(grad_ref[u], qs[u], 1, 0))
+        place_unit(value_part, 0, u, everything, contract(prob, gs[u], 1, 0))
+        place_unit(key_part, 0, u, everything, contract(grad, qs[u], 1, 0))
     for part, total in ((key_part, key_sum), (value_part, value_sum)):
         for i in range(C):
             here = jnp.where(meta_ref[PREV + i] == i, part[i, tokens:], 0.0)
@@ -405,25 +460,29 @@
     theirs = swap(send)
     wide = jax.ShapeDtypeStruct((UNITS, UNIT // 2, UNIT), BF16)
     rows = jax.ShapeDtypeStruct((UNITS, tokens, UNIT), BF16)
-    half = jax.ShapeDtypeStruct((UNITS, tokens, UNIT // 2), F32)
+    lanes = UNIT // 2
+    half = jax.ShapeDtypeStruct((UNITS, tokens, lanes), F32)
+    tall = jax.ShapeDtypeStruct((UNITS, UNIT, lanes), BF16)
+    few = jax.ShapeDtypeStruct((UNITS, 8, lanes), F32)
     local = call(
         local_kernel,
         (meta, mine, theirs),
-        (wide, wide, rows, rows, rows, rows, half, half),
+        (wide, wide, rows, rows, rows, rows, half, half, few, tall, tall),
         [SMEM] + [VMEM] * 2,
-        (VMEM,) * 8,
+        (VMEM,) * 11,
         [pltpu.VMEM((4, C, tokens, SPAN), BF16)],
         size=4 << 20,
     )
-    soft = jax.ShapeDtypeStruct((UNITS, 2 * tokens, UNIT // 2), BF16)
+    soft = jax.ShapeDtypeStruct((UNITS, tokens, lanes), BF16)
+    first = jax.ShapeDtypeStruct((2, 2, tokens, lanes), BF16)
     flops = 24 * C * tokens * tokens * SPAN
-    sums, edge_sums, prob, grad_score = call(
+    sums, edge_sums, *softened = call(
         near_kernel,
-        (meta, *received, *local),
-        (shape(2, SPAN), shape(4, SPAN), soft, soft),
-        [SMEM] + [VMEM] * 11,
-        (VMEM,) * 4,
-        [pltpu.VMEM((UNITS, 2 * tokens, UNIT // 2), F32)] * 2,
+        (meta, *received, *local[:6], *local[8:]),
+        (shape(2, SPAN), shape(4, SPAN), soft, soft, first, few),
+        [SMEM] + [VMEM] * 12,
+        (VMEM,) * 6,
+        [],
         flops,
         2 << 20,
     )
@@ -431,9 +490,9 @@
     returned = (ring(edge_sums, -2), far[1], far[0])
     keep, send_out, touch = call(
         full_kernel,
-        (meta, *received, *local[:6], prob, grad_score),
+        (meta, *received, *local[:8], *softened),
         (shape(4 * F, SPAN), shape(4 * F, REST), shape(4, SPAN, F32)),
-        [SMEM] + [VMEM] * 11,
+        [SMEM] + [VMEM] * 15,
         (VMEM,) * 3,
         [room(4 * C)]
         + [pltpu.VMEM((C, 2 * tokens, SPAN), F32)] * 2

time: 37.8 us -> 37.5 us (level)
  no operation moved by 1% of the time
where the time goes in v2:
time: 37.5 us; the launch traced here: 37.3 us
  starting transfers between devices  15.1 us (40%)
  waiting for transfers between devices  11.7 us (31%)
  Pallas kernels  9.78 us (26%)
  between operations  0.68 us (2%)
    ppermute x6, waiting for transfers between devices, ring(): lax.ppermute(value, 'tm', [(s, (s + steps) % count) for s in range(count)])  10.6 us
    pallas_call x8, Pallas kernels, call(): pl.pallas_call(kernel, out_shape=outs, in_specs=in_specs, out_specs=out_s...  9.78 us
    ppermute x6, starting transfers between devices, ring(): lax.ppermute(value, 'tm', [(s, (s + steps) % count) for s in range(count)])  8.23 us
    ppermute x4, starting transfers between devices, swap(): return lax.ppermute(value, 'tm', [(s, s ^ 1) for s in range(count)])  6.9 us
    ppermute x4, waiting for transfers between devices, swap(): return lax.ppermute(value, 'tm', [(s, s ^ 1) for s in range(count)])  1.07 us
  transfers between devices with their start and end apart: 10, of which 6 were waited for; matrix products, arithmetic and copies ran while one was open for 0% of the time, Pallas kernels for 7%

profile of v2, /device:TPU:1, one launch (start us, length us, event | category | flops | bytes accessed | tf_op | source)
XLA Modules:
  0.0 37.3 jit_solution(13246266215394753506)
XLA Ops:
  0.6 1.7 %shard_map.84 = (s32[21]{0:T(128)S(1)}, bf16[4,32,384]{2,1,0:T(8,128)(2,1)S(1)}, bf16[4,32,384]{2,1,0:T(8,128)(2,1)S(1)}) custom-call(s32[1,128]{1,0:T(1,128)} %bitcast.1, bf16[4,32,640]{2,1,0:T(8,128)(2,1)} %keys_ref.3, bf16[4,32,640]{2,1,0:T(8,128)(2,1)} %values_ref.3), custom_call_target="tpu_custom_call" | custom-call | bytes 1048576 | tf_op jit(solution)/shard_map/pallas_call | solution.py:410
  2.3 3.3 %collective-permute-start = (bf16[4,32,384]{2,1,0:T(8,128)(2,1)S(1)}, bf16[4,32,384]{2,1,0:T(8,128)(2,1)S(1)}, u32[]{:S(2)}, u32[]{:S(2)}) collective-permute-start(bf16[4,32,384]{2,1,0:T(8,128)(2,1)S(1)} %get-tuple-element.37), channel_id=1, source_target_pairs={{0,1},{1,0},{2,3},{3,2},{4,5},{5,4},{6,7},{7,6},{8,9},{9,8},{10,11... | collective-permute-start | bytes 294920 | tf_op jit(solution)/shard_map/ppermute | solution.py:38
  5.6 0.9 %collective-permute-done = bf16[4,32,384]{2,1,0:T(8,128)(2,1)S(1)} collective-permute-done((bf16[4,32,384]{2,1,0:T(8,128)(2,1)S(1)}, bf16[4,32,384]{2,1,0:T(8,128)(2,1)S(1)}, u32[]{:S(2)}, u32[]{:S(2)}) %collective-permute-start) | collective-permute-done | bytes 98336 | tf_op jit(solution)/shard_map/ppermute | solution.py:38
  6.6 1.3 %shard_map.85 = (bf16[16,32,384]{2,1,0:T(8,128)(2,1)S(1)}, bf16[16,32,384]{2,1,0:T(8,128)(2,1)S(1)}) custom-call(bf16[4,32,640]{2,1,0:T(8,128)(2,1)} %q_ref.1, bf16[4,32,640]{2,1,0:T(8,128)(2,1)} %keys_ref.3, bf16[4,32,640]{2,1,0:T(8,128)(2,1)} %values_ref.3, bf16[4,32,640]{2,1,0:T(8,128)(2,1)} %g_ref.1, bf16[4,32,384]{2,1,0:T(8,128)(2,1)S(1)} %add.6.after_ref), custom_call_target="tpu_custom_call" | custom-call | bytes 2097152 | tf_op jit(solution)/shard_map/pallas_call | solution.py:410
  7.9 0.4 %collective-permute-start.4 = (bf16[16,32,384]{2,1,0:T(8,128)(2,1)S(1)}, bf16[16,32,384]{2,1,0:T(8,128)(2,1)S(1)}, u32[]{:S(2)}, u32[]{:S(2)}) collective-permute-start(bf16[16,32,384]{2,1,0:T(8,128)(2,1)S(1)} %get-tuple-element.39), channel_id=1, source_target_pairs={{0,1},{1,0},{2,3},{3,2},{4,5},{5,4},{6,7},{7,6},{8,9},{9,8},{10,11... | collective-permute-start | bytes 1179656 | tf_op jit(solution)/shard_map/ppermute | solution.py:38
  8.3 0.0 collective-permute-start.1
  8.3 2.1 %collective-permute-start.3 = (bf16[2,32,384]{2,1,0:T(8,128)(2,1)S(1)}, bf16[2,32,384]{2,1,0:T(8,128)(2,1)S(1)}, u32[]{:S(2)}, u32[]{:S(2)}) collective-permute-start(bf16[2,32,384]{2,1,0:T(8,128)(2,1)S(1)} %slice_add_fusion), channel_id=1, source_target_pairs={{0,6},{1,7},{2,8},{3,9},{4,10},{5,11},{6,12},{7,13},{8,14},{9,15},... | collective-permute-start | bytes 147464 | tf_op jit(solution)/shard_map/ppermute | solution.py:33
  10.4 1.5 %collective-permute-start.2 = (bf16[2,32,384]{2,1,0:T(8,128)(2,1)S(1)}, bf16[2,32,384]{2,1,0:T(8,128)(2,1)S(1)}, u32[]{:S(2)}, u32[]{:S(2)}) collective-permute-start(bf16[2,32,384]{2,1,0:T(8,128)(2,1)S(1)} %slice_add_fusion), channel_id=1, source_target_pairs={{0,4},{1,5},{2,6},{3,7},{4,8},{5,9},{6,10},{7,11},{8,12},{9,13},{1... | collective-permute-start | bytes 147464 | tf_op jit(solution)/shard_map/ppermute | solution.py:33
  11.9 0.0 collective-permute-done.4.theirs_ref
  11.9 1.3 %shard_map.86 = (bf16[12,128,256]{2,1,0:T(8,128)(2,1)S(1)}, bf16[12,128,256]{2,1,0:T(8,128)(2,1)S(1)}, bf16[12,32,256]{2,1,0:T(8,128)(2,1)S(1)}, bf16[12,32,256]...) custom-call(s32[21]{0:T(128)S(1)} %get-tuple-element.35.meta_ref, ...), custom_call_target="tpu_custom_call" | custom-call | bytes 4194304 | tf_op jit(solution)/shard_map/pallas_call | solution.py:410
  13.2 5.6 %collective-permute-done.3.r3 = bf16[2,32,384]{2,1,0:T(8,128)(2,1)S(1)} collective-permute-done((bf16[2,32,384]{2,1,0:T(8,128)(2,1)S(1)}, bf16[2,32,384]{2,1,0:T(8,128)(2,1)S(1)}, u32[]{:S(2)}, u32[]{:S(2)}) %collective-permute-start.3) | collective-permute-done | bytes 49184 | tf_op jit(solution)/shard_map/ppermute | solution.py:33
  18.8 2.6 %collective-permute-done.2.r2 = bf16[2,32,384]{2,1,0:T(8,128)(2,1)S(1)} collective-permute-done((bf16[2,32,384]{2,1,0:T(8,128)(2,1)S(1)}, bf16[2,32,384]{2,1,0:T(8,128)(2,1)S(1)}, u32[]{:S(2)}, u32[]{:S(2)}) %collective-permute-start.2) | collective-permute-done | bytes 49184 | tf_op jit(solution)/shard_map/ppermute | solution.py:33
  21.4 0.0 collective-permute-done.1.r1
  21.5 1.2 %shard_map.87 = (bf16[2,32,384]{2,1,0:T(8,128)(2,1)S(1)}, bf16[4,32,384]{2,1,0:T(8,128)(2,1)S(1)}, bf16[12,32,128]{2,1,0:T(8,128)(2,1)S(1)}, bf16[12,32,128]{2,1...) custom-call(s32[21]{0:T(128)S(1)} %get-tuple-element.35.meta_ref, ...), custom_call_target="tpu_custom_call" | custom-call | flops 75497472 | bytes 2097152 | tf_op jit(solution)/shard_map/pallas_call | solution.py:410
  22.7 1.5 %shard_map.88 = (bf16[16,32,384]{2,1,0:T(8,128)(2,1)S(1)}, bf16[16,32,256]{2,1,0:T(8,128)(2,1)S(1)}, f32[4,32,384]{2,1,0:T(8,128)S(1)}) custom-call(s32[21]{0:T(128)S(1)} %get-tuple-element.35.meta_ref, bf16[4,32,384]{2,1,0:T(8,128)(2,1)S(1)} %collective-permute-done.1.r1, bf16[2,32,384]{2,1,0:T(8,128)(2,1)S(1)} %collective-permute-done.2.r2, ...), custom_call_target="tpu_custom_call" | custom-call | flops 301989888 | bytes 4194304 | tf_op jit(solution)/shard_map/pallas_call | solution.py:410
  24.2 1.3 %collective-permute-start.5 = (bf16[16,32,256]{2,1,0:T(8,128)(2,1)S(1)}, bf16[16,32,256]{2,1,0:T(8,128)(2,1)S(1)}, u32[]{:S(2)}, u32[]{:S(2)}) collective-permute-start(bf16[16,32,256]{2,1,0:T(8,128)(2,1)S(1)} %get-tuple-element.56), channel_id=1, source_target_pairs={{0,1},{1,0},{2,3},{3,2},{4,5},{5,4},{6,7},{7,6},{8,9},{9,8},{10,11... | collective-permute-start | bytes 786440 | tf_op jit(solution)/shard_map/ppermute | solution.py:38
  25.5 1.0 %collective-permute-start.6 = (bf16[4,32,384]{2,1,0:T(8,128)(2,1)S(1)}, bf16[4,32,384]{2,1,0:T(8,128)(2,1)S(1)}, u32[]{:S(2)}, u32[]{:S(2)}) collective-permute-start(bf16[4,32,384]{2,1,0:T(8,128)(2,1)S(1)} %get-tuple-element.60), channel_id=1, source_target_pairs={{0,254},{1,255},{2,0},{3,1},{4,2},{5,3},{6,4},{7,5},{8,6},{9,7},{1... | collective-permute-start | bytes 294920 | tf_op jit(solution)/shard_map/ppermute | solution.py:33
  26.6 1.6 %collective-permute-start.8 = (bf16[2,32,384]{2,1,0:T(8,128)(2,1)S(1)}, bf16[2,32,384]{2,1,0:T(8,128)(2,1)S(1)}, u32[]{:S(2)}, u32[]{:S(2)}) collective-permute-start(bf16[2,32,384]{2,1,0:T(8,128)(2,1)S(1)} %get-tuple-element.61), channel_id=1, source_target_pairs={{0,250},{1,251},{2,252},{3,253},{4,254},{5,255},{6,0},{7,1},{8,2},... | collective-permute-start | bytes 147464 | tf_op jit(solution)/shard_map/ppermute | solution.py:33
  28.1 2.0 %collective-permute-start.7 = (bf16[2,32,384]{2,1,0:T(8,128)(2,1)S(1)}, bf16[2,32,384]{2,1,0:T(8,128)(2,1)S(1)}, u32[]{:S(2)}, u32[]{:S(2)}) collective-permute-start(bf16[2,32,384]{2,1,0:T(8,128)(2,1)S(1)} %get-tuple-element.61), channel_id=1, source_target_pairs={{0,252},{1,253},{2,254},{3,255},{4,0},{5,1},{6,2},{7,3},{8,4},{9,5... | collective-permute-start | bytes 147464 | tf_op jit(solution)/shard_map/ppermute | solution.py:33
  30.2 0.6 %collective-permute-done.8.r3 = bf16[2,32,384]{2,1,0:T(8,128)(2,1)S(1)} collective-permute-done((bf16[2,32,384]{2,1,0:T(8,128)(2,1)S(1)}, bf16[2,32,384]{2,1,0:T(8,128)(2,1)S(1)}, u32[]{:S(2)}, u32[]{:S(2)}) %collective-permute-start.8) | collective-permute-done | bytes 49184 | tf_op jit(solution)/shard_map/ppermute | solution.py:33
  30.7 1.9 %collective-permute-done.7.r2 = bf16[2,32,384]{2,1,0:T(8,128)(2,1)S(1)} collective-permute-done((bf16[2,32,384]{2,1,0:T(8,128)(2,1)S(1)}, bf16[2,32,384]{2,1,0:T(8,128)(2,1)S(1)}, u32[]{:S(2)}, u32[]{:S(2)}) %collective-permute-start.7) | collective-permute-done | bytes 49184 | tf_op jit(solution)/shard_map/ppermute | solution.py:33
  32.6 0.0 collective-permute-done.6.r1
  32.6 0.6 %shard_map.90 = (bf16[4,32,384]{2,1,0:T(8,128)(2,1)S(1)}, bf16[4,32,256]{2,1,0:T(8,128)(2,1)S(1)}) custom-call(s32[21]{0:T(128)S(1)} %get-tuple-element.35.meta_ref, f32[4,32,384]{2,1,0:T(8,128)S(1)} %get-tuple-element.59.touch_ref, bf16[4,32,384]{2,1,0:T(8,128)(2,1)S(1)} %collective-permute-done.6.r1, bf16[2,32,384]{2,1,0:T(8,128)(2,1)S(1)} %collective-permute-done.7.r2, ...), custom_call_target="tpu_custom_call" | custom-call | bytes 1048576 | tf_op jit(solution)/shard_map/pallas_call | solution.py:410
  33.2 1.9 %collective-permute-start.9 = (bf16[4,32,256]{2,1,0:T(8,128)(2,1)S(1)}, bf16[4,32,256]{2,1,0:T(8,128)(2,1)S(1)}, u32[]{:S(2)}, u32[]{:S(2)}) collective-permute-start(bf16[4,32,256]{2,1,0:T(8,128)(2,1)S(1)} %get-tuple-element.63), channel_id=1, source_target_pairs={{0,1},{1,0},{2,3},{3,2},{4,5},{5,4},{6,7},{7,6},{8,9},{9,8},{10,11... | collective-permute-start | bytes 196616 | tf_op jit(solution)/shard_map/ppermute | solution.py:38
  35.1 0.0 collective-permute-done.5.got_ref
  35.1 0.8 %shard_map.89 = (bf16[4,32,640]{2,1,0:T(8,128)(2,1)}, bf16[4,32,640]{2,1,0:T(8,128)(2,1)}) custom-call(bf16[16,32,384]{2,1,0:T(8,128)(2,1)S(1)} %get-tuple-element.55.keep_ref, bf16[16,32,256]{2,1,0:T(8,128)(2,1)S(1)} %collective-permute-done.5.got_ref), custom_call_target="tpu_custom_call" | custom-call | bytes 1048576 | tf_op jit(solution)/shard_map/pallas_call | solution.py:410
  35.9 0.1 collective-permute-done.9.touched_got_ref
  36.0 1.4 %shard_map.91 = (bf16[4,32,640]{2,1,0:T(8,128)(2,1)}, bf16[4,32,640]{2,1,0:T(8,128)(2,1)}) custom-call(s32[21]{0:T(128)S(1)} %get-tuple-element.35.meta_ref, bf16[16,32,384]{2,1,0:T(8,128)(2,1)S(1)} %get-tuple-element.55.keep_ref, bf16[16,32,256]{2,1,0:T(8,128)(2,1)S(1)} %collective-permute-done.5.got_ref, ...), custom_call_target="tpu_custom_call" | custom-call | bytes 1048576 | tf_op jit(solution)/shard_map/pallas_call | solution.py:410
  (2 shorter events, 0.0 us)
Async XLA Ops:
  2.3 4.2 %collective-permute-start = (bf16[4,32,384]{2,1,0:T(8,128)(2,1)S(1)}, bf16[4,32,384]{2,1,0:T(8,128)(2,1)S(1)}, u32[]{:S(2)}, u32[]{:S(2)}) collective-permute-start(bf16[4,32,384]{2,1,0:T(8,128)(2,1)S(1)} %get-tuple-element.37), channel_id=1, source_target_pairs={{0,1},{1,0},{2,3},{3,2},{4,5},{5,4},{6,7},{7,6},{8,9},{9,8},{10,11... | collective-permute-start | bytes 294920 | tf_op jit(solution)/shard_map/ppermute | solution.py:38
  7.9 4.1 %collective-permute-start.4 = (bf16[16,32,384]{2,1,0:T(8,128)(2,1)S(1)}, bf16[16,32,384]{2,1,0:T(8,128)(2,1)S(1)}, u32[]{:S(2)}, u32[]{:S(2)}) collective-permute-start(bf16[16,32,384]{2,1,0:T(8,128)(2,1)S(1)} %get-tuple-element.39), channel_id=1, source_target_pairs={{0,1},{1,0},{2,3},{3,2},{4,5},{5,4},{6,7},{7,6},{8,9},{9,8},{10,11... | collective-permute-start | bytes 1179656 | tf_op jit(solution)/shard_map/ppermute | solution.py:38
  8.3 13.2 %collective-permute-start.1 = (bf16[4,32,384]{2,1,0:T(8,128)(2,1)S(1)}, bf16[4,32,384]{2,1,0:T(8,128)(2,1)S(1)}, u32[]{:S(2)}, u32[]{:S(2)}) collective-permute-start(bf16[4,32,384]{2,1,0:T(8,128)(2,1)S(1)} %add.6.after_ref), channel_id=1, source_target_pairs={{0,2},{1,3},{2,4},{3,5},{4,6},{5,7},{6,8},{7,9},{8,10},{9,11},{10,... | collective-permute-start | bytes 294920 | tf_op jit(solution)/shard_map/ppermute | solution.py:33
  8.3 10.5 %collective-permute-start.3 = (bf16[2,32,384]{2,1,0:T(8,128)(2,1)S(1)}, bf16[2,32,384]{2,1,0:T(8,128)(2,1)S(1)}, u32[]{:S(2)}, u32[]{:S(2)}) collective-permute-start(bf16[2,32,384]{2,1,0:T(8,128)(2,1)S(1)} %slice_add_fusion), channel_id=1, source_target_pairs={{0,6},{1,7},{2,8},{3,9},{4,10},{5,11},{6,12},{7,13},{8,14},{9,15},... | collective-permute-start | bytes 147464 | tf_op jit(solution)/shard_map/ppermute | solution.py:33
  10.4 11.1 %collective-permute-start.2 = (bf16[2,32,384]{2,1,0:T(8,128)(2,1)S(1)}, bf16[2,32,384]{2,1,0:T(8,128)(2,1)S(1)}, u32[]{:S(2)}, u32[]{:S(2)}) collective-permute-start(bf16[2,32,384]{2,1,0:T(8,128)(2,1)S(1)} %slice_add_fusion), channel_id=1, source_target_pairs={{0,4},{1,5},{2,6},{3,7},{4,8},{5,9},{6,10},{7,11},{8,12},{9,13},{1... | collective-permute-start | bytes 147464 | tf_op jit(solution)/shard_map/ppermute | solution.py:33
  24.2 10.9 %collective-permute-start.5 = (bf16[16,32,256]{2,1,0:T(8,128)(2,1)S(1)}, bf16[16,32,256]{2,1,0:T(8,128)(2,1)S(1)}, u32[]{:S(2)}, u32[]{:S(2)}) collective-permute-start(bf16[16,32,256]{2,1,0:T(8,128)(2,1)S(1)} %get-tuple-element.56), channel_id=1, source_target_pairs={{0,1},{1,0},{2,3},{3,2},{4,5},{5,4},{6,7},{7,6},{8,9},{9,8},{10,11... | collective-permute-start | bytes 786440 | tf_op jit(solution)/shard_map/ppermute | solution.py:38
  25.5 7.1 %collective-permute-start.6 = (bf16[4,32,384]{2,1,0:T(8,128)(2,1)S(1)}, bf16[4,32,384]{2,1,0:T(8,128)(2,1)S(1)}, u32[]{:S(2)}, u32[]{:S(2)}) collective-permute-start(bf16[4,32,384]{2,1,0:T(8,128)(2,1)S(1)} %get-tuple-element.60), channel_id=1, source_target_pairs={{0,254},{1,255},{2,0},{3,1},{4,2},{5,3},{6,4},{7,5},{8,6},{9,7},{1... | collective-permute-start | bytes 294920 | tf_op jit(solution)/shard_map/ppermute | solution.py:33
  26.6 4.2 %collective-permute-start.8 = (bf16[2,32,384]{2,1,0:T(8,128)(2,1)S(1)}, bf16[2,32,384]{2,1,0:T(8,128)(2,1)S(1)}, u32[]{:S(2)}, u32[]{:S(2)}) collective-permute-start(bf16[2,32,384]{2,1,0:T(8,128)(2,1)S(1)} %get-tuple-element.61), channel_id=1, source_target_pairs={{0,250},{1,251},{2,252},{3,253},{4,254},{5,255},{6,0},{7,1},{8,2},... | collective-permute-start | bytes 147464 | tf_op jit(solution)/shard_map/ppermute | solution.py:33
  28.1 4.4 %collective-permute-start.7 = (bf16[2,32,384]{2,1,0:T(8,128)(2,1)S(1)}, bf16[2,32,384]{2,1,0:T(8,128)(2,1)S(1)}, u32[]{:S(2)}, u32[]{:S(2)}) collective-permute-start(bf16[2,32,384]{2,1,0:T(8,128)(2,1)S(1)} %get-tuple-element.61), channel_id=1, source_target_pairs={{0,252},{1,253},{2,254},{3,255},{4,0},{5,1},{6,2},{7,3},{8,4},{9,5... | collective-permute-start | bytes 147464 | tf_op jit(solution)/shard_map/ppermute | solution.py:33
  33.2 2.8 %collective-permute-start.9 = (bf16[4,32,256]{2,1,0:T(8,128)(2,1)S(1)}, bf16[4,32,256]{2,1,0:T(8,128)(2,1)S(1)}, u32[]{:S(2)}, u32[]{:S(2)}) collective-permute-start(bf16[4,32,256]{2,1,0:T(8,128)(2,1)S(1)} %get-tuple-element.63), channel_id=1, source_target_pairs={{0,1},{1,0},{2,3},{3,2},{4,5},{5,4},{6,7},{7,6},{8,9},{9,8},{10,11... | collective-permute-start | bytes 196616 | tf_op jit(solution)/shard_map/ppermute | solution.py:38
